TPU v7x, 256 devices: a whole 4x4x8 slice. The times are simulated.
256 devices in a mesh: attn: 32 (over y, z), proj: 8 (over x, core).
Axes of the slice: x: 4, y: 4, z: 8, core: 2. Of those that a mesh axis runs over, the one named last changes fastest.
Arguments:
- tokens: bfloat16 [16384, 4096], P('attn', 'proj'), may hold values from -6 to 6
- norm_gain: float32 [4096], replicated, may hold values from 0.1 to 1.9
- w_query: bfloat16 [4096, 4096], P(None, 'proj')
- w_key: bfloat16 [4096, 1024], P(None, 'proj')
- value_matrix: bfloat16 [4096, 1024], P(None, 'proj'), may hold values from -0.09375 to 0.09375
- doc_lengths: int32 [128], replicated, may hold values from 1 to 512, 16384 in all
- block_server: int32 [128], P('attn'), may hold values from 0 to 31, as said below
Outputs:
- attn_out: bfloat16 [16384, 4096], P('attn', 'proj')
- served_lse: float32 [128, 32, 128], P('attn', 'proj')
Inputs may be any that keep to these rules, and one draw needn't show every extreme that they name: `doc_lengths`: the lengths sum to 16384. `block_server`: query block b belongs to the micro-batch b // 4; every index of attn serves exactly 4 blocks, and at most one block of any one micro-batch.
All inputs are finite; a program needn't handle non-finite values.
Results may differ from a plain program's by a relative error of at most 0.0074.
Values may be sent and summed in bfloat16 or wider, within the bound.
A program may use at most 128 MiB of HBM per device.

v0:
```python
import jax
import jax.numpy as jnp
from jax import lax
from jax.sharding import PartitionSpec as P

HEAD_SIZE = 128
QUERY_BLOCK_ROWS = 128


big_value = 1e30
norm_eps = 1e-05


def row_first(starts, position):
    return jnp.max(jnp.where(starts[None, :] <= position[:, None], starts[None, :], 0), axis=1)


def empty_state(kv_heads, group):
    running = jnp.full((kv_heads, group, QUERY_BLOCK_ROWS), -big_value, jnp.float32)
    total = jnp.zeros((kv_heads, group, QUERY_BLOCK_ROWS), jnp.float32)
    summed = jnp.zeros((kv_heads, group, QUERY_BLOCK_ROWS, HEAD_SIZE), jnp.float32)
    return (running, total, summed)


def attend(state, query_block, first_row, keys_values, key_start, starts, window):
    width = keys_values.shape[1] // 2
    kv_heads = width // HEAD_SIZE
    group = query_block.shape[1] // (kv_heads * HEAD_SIZE)
    count = keys_values.shape[0]
    row_extent = min(window, count)
    lowest = row_first(starts, first_row[None])[0]
    touches = (lowest < key_start + count) & (first_row + QUERY_BLOCK_ROWS > key_start)

    def update(current):
        running, total, summed = current
        offset = jnp.clip(lowest, 0, count - row_extent)
        rows_kv = lax.dynamic_slice_in_dim(keys_values, offset, row_extent, 0)
        key_pos = offset + jnp.arange(row_extent, dtype=jnp.int32)
        query_pos = first_row + jnp.arange(QUERY_BLOCK_ROWS, dtype=jnp.int32)
        bounds = row_first(starts, query_pos)
        allowed = (key_pos[None, :] >= bounds[:, None]) & (key_pos[None, :] <= query_pos[:, None])
        query_vectors = query_block.reshape(QUERY_BLOCK_ROWS, kv_heads, group, HEAD_SIZE)
        keys = rows_kv[:, :width].reshape(row_extent, kv_heads, HEAD_SIZE)
        values = rows_kv[:, width:].reshape(row_extent, kv_heads, HEAD_SIZE)
        scores = jnp.einsum(
            "qngd,knd->ngqk", query_vectors, keys, preferred_element_type=jnp.float32
        ) * (1.0 / HEAD_SIZE**0.5)
        scores = jnp.where(allowed, scores, -big_value)
        highest = jnp.maximum(running, jnp.max(scores, axis=-1))
        weights = jnp.where(allowed, jnp.exp(scores - highest[..., None]), 0.0)
        total = jnp.sum(weights, axis=-1)
        summed = jnp.einsum(
            "ngqk,knd->ngqd",
            weights.astype(jnp.bfloat16),
            values,
            preferred_element_type=jnp.float32,
        )
        return (highest, total, summed)

    return lax.cond(touches, update, lambda current: current, state)


def finish(state):
    running, total, summed = state
    result = summed / total[..., None]
    kv_heads, group = (result.shape[0], result.shape[1])
    result = (
        jnp.transpose(result, (2, 0, 1, 3))
        .reshape(QUERY_BLOCK_ROWS, kv_heads * group * HEAD_SIZE)
        .astype(jnp.bfloat16)
    )
    lse = (running + jnp.log(total)).reshape(kv_heads * group, QUERY_BLOCK_ROWS)
    return (result, lse)


def shards(tokens, norm_gain, w_query, w_key, value_matrix, doc_lengths, block_server):
    rows = tokens.shape[0]
    model_width = w_query.shape[0]
    query_width = w_query.shape[1]
    key_width = w_key.shape[1]
    kv_heads = key_width // HEAD_SIZE
    group = query_width // key_width
    blocks = rows // QUERY_BLOCK_ROWS
    servers = lax.axis_size("attn")
    me_attn = lax.axis_index("attn")
    wide = lax.all_gather(tokens, "proj", axis=1, tiled=True).astype(jnp.float32)
    scaled = (wide * norm_gain[None, :]).astype(jnp.bfloat16)
    part_q = jnp.dot(scaled, w_query, preferred_element_type=jnp.float32)
    part_k = jnp.dot(scaled, w_key, preferred_element_type=jnp.float32)
    part_v = jnp.dot(scaled, value_matrix, preferred_element_type=jnp.float32)
    squares = jnp.sum(wide * wide, axis=1, keepdims=True)
    part_q, part_k, part_v, squares = (part_q, part_k, part_v, squares)
    inverse = lax.rsqrt(squares / model_width + norm_eps)
    query_vectors = (part_q * inverse).astype(jnp.bfloat16)
    keys_values = jnp.concatenate(
        [(part_k * inverse).astype(jnp.bfloat16), (part_v * inverse).astype(jnp.bfloat16)], axis=1
    )
    ends = jnp.cumsum(doc_lengths)
    starts = ends - doc_lengths
    window = rows + QUERY_BLOCK_ROWS
    slot_ids = jnp.arange(servers, dtype=jnp.int32)
    sending = block_server[None, :] == slot_ids[:, None]
    global_ids = me_attn * blocks + jnp.arange(blocks, dtype=jnp.int32)
    send_id = (jnp.sum(jnp.where(sending, global_ids[None, :] + 1, 0), axis=1) - 1).reshape(
        servers, 1
    )
    query_blocks = query_vectors.reshape(blocks, QUERY_BLOCK_ROWS * query_width)
    send_q = (
        jnp.dot(sending.astype(jnp.bfloat16), query_blocks, preferred_element_type=jnp.float32)
        .astype(jnp.bfloat16)
        .reshape(servers, QUERY_BLOCK_ROWS, query_width)
    )
    recv_q, recv_id = (
        lax.all_to_all(send_q, "attn", split_axis=0, concat_axis=0, tiled=True),
        lax.all_to_all(send_id, "attn", split_axis=0, concat_axis=0, tiled=True),
    )
    valid = recv_id[:, 0] >= 0
    ranks = jnp.cumsum(valid.astype(jnp.int32)) - 1
    picking = (ranks[None, :] == jnp.arange(blocks, dtype=jnp.int32)[:, None]) & valid[None, :]
    my_queries = (
        jnp.dot(
            picking.astype(jnp.bfloat16),
            recv_q.reshape(servers, QUERY_BLOCK_ROWS * query_width),
            preferred_element_type=jnp.float32,
        )
        .astype(jnp.bfloat16)
        .reshape(blocks, QUERY_BLOCK_ROWS, query_width)
    )
    my_ids = jnp.sum(jnp.where(picking, recv_id[:, 0][None, :], 0), axis=1).astype(jnp.int32)
    states = tuple((empty_state(kv_heads, group) for index in range(blocks)))
    piece = lax.all_gather(keys_values, "attn", axis=0, tiled=True)
    start = jnp.int32(0)
    states = tuple(
        (
            attend(
                states[index],
                my_queries[index],
                my_ids[index] * QUERY_BLOCK_ROWS,
                piece,
                start,
                starts,
                window,
            )
            for index in range(blocks)
        )
    )
    finished = [finish(state) for state in states]
    outputs = jnp.stack([item[0] for item in finished]).reshape(
        blocks, QUERY_BLOCK_ROWS * query_width
    )
    served_lse = jnp.stack([item[1] for item in finished])
    back = (
        jnp.dot(picking.T.astype(jnp.bfloat16), outputs, preferred_element_type=jnp.float32)
        .astype(jnp.bfloat16)
        .reshape(servers, QUERY_BLOCK_ROWS, query_width)
    )
    returned = lax.all_to_all(back, "attn", split_axis=0, concat_axis=0, tiled=True)
    attn_out = (
        jnp.dot(
            sending.T.astype(jnp.bfloat16),
            returned.reshape(servers, QUERY_BLOCK_ROWS * query_width),
            preferred_element_type=jnp.float32,
        )
        .astype(jnp.bfloat16)
        .reshape(rows, query_width)
    )
    return (attn_out, served_lse)


def solution(mesh):
    return jax.shard_map(
        shards,
        mesh=mesh,
        in_specs=(
            P("attn", "proj"),
            P(),
            P(None, "proj"),
            P(None, "proj"),
            P(None, "proj"),
            P(),
            P("attn"),
        ),
        out_specs=(P("attn", "proj"), P("attn", "proj", None)),
        check_vma=False,
    )
```

profile of v0, /device:TPU:2, one launch (start us, length us, event | category | flops | bytes accessed | tf_op | source)
XLA Modules:
  0.0 423.8 jit_solution(2424026122402465434)
XLA Ops:
  8.0 38.4 %all-gather.3.cloned.1.call-done = bf16[512,4096]{1,0:T(8,128)(2,1)} async-done(((bf16[512,512]{1,0:T(8,128)(2,1)}), bf16[512,4096]{1,0:T(8,128)(2,1)}) %all-gather.3.cloned.1.call-update) | async-done | bytes 4194320 | tf_op jit(solution)/shard_map/all_gather | solution.py:86
  46.4 3.2 fusion.49
  49.8 1.5 fusion.68
  51.4 1.5 fusion.71
  54.5 9.9 %all-to-all-start = ((s32[32,1,1]{2,1,0:T(1,128)}), s32[32,1,1]{2,1,0:T(1,128)S(1)}, u32[]{:S(2)}, u32[]{:S(2)}) async-start(s32[32,1,1]{2,1,0:T(1,128)} %copy.83), calls=%async_computation | async-start | bytes 32768 | tf_op jit(solution)/shard_map/all_to_all | solution.py:115
  64.3 5.9 %fusion.59 = bf16[512,512]{1,0:T(8,128)(2,1)S(1)} fusion(bf16[4096,512]{1,0:T(8,128)(2,1)} %param.17, bf16[512,4096]{1,0:T(8,128)(2,1)} %all-gather.3.cloned.1.call-done, f32[4096]{0:T(1024)S(1)} %copy-done.6, f32[512]{0:T(512)S(1)} %add_rsqrt_fusion), kind=kOutput, calls=%fused_computation.104 | convolution fusion | flops 2154299392 | bytes 8931328 | tf_op jit(solution)/shard_map/dot_general | solution.py:88
  70.7 1.4 convolution_convert_fusion.1
  72.0 3.5 copy.106
  75.5 10.2 %all-to-all-start.1 = ((bf16[32,128,512]{2,1,0:T(8,128)(2,1)}), bf16[32,128,512]{2,1,0:T(8,128)(2,1)}, u32[]{:S(2)}, u32[]{:S(2)}) async-start(bf16[32,128,512]{2,1,0:T(8,128)(2,1)} %bitcast.167), calls=%async_computation.1 | async-start | bytes 8388608 | tf_op jit(solution)/shard_map/all_to_all | solution.py:114
  90.3 0.8 fusion.88
  93.6 107.1 %all-to-all-done.1 = bf16[32,128,512]{2,1,0:T(8,128)(2,1)} async-done(((bf16[32,128,512]{2,1,0:T(8,128)(2,1)}), bf16[32,128,512]{2,1,0:T(8,128)(2,1)}, u32[]{:S(2)}, u32[]{:S(2)}) %all-to-all-start.1) | async-done | bytes 4194336 | tf_op jit(solution)/shard_map/all_to_all | solution.py:114
  200.7 4.6 %copy.107 = bf16[4,8,128,512]{3,1,2,0:T(8,128)(2,1)S(1)} copy(bf16[4,8,128,512]{3,2,1,0:T(8,128)(2,1)} %bitcast.85) | data formatting | bytes 8388608
  206.0 20.7 %all-gather.5.cloned.1.call-done = bf16[16384,256]{0,1:T(8,128)(2,1)} async-done(((bf16[512,256]{0,1:T(8,128)(2,1)}), bf16[16384,256]{0,1:T(8,128)(2,1)}) %all-gather.5.cloned.1.call-update) | async-done | bytes 8388624 | tf_op jit(solution)/shard_map/all_gather | solution.py:131
  226.7 17.9 %conditional.4 = (f32[1,4,128]{2,1,0:T(4,128)}, f32[1,4,128,128]{3,2,1,0:T(8,128)S(1)}, f32[1,4,128]{2,1,0:T(4,128)S(1)}) conditional(s32[]{:T(128)} %convert_element_type.140, () %tuple.40, (s32[]{:T(128)}, s32[128]{0:T(128)S(1)}, s32[]{:T(128)}, bf16[16384,256]{0,1:T(8,128)(2,1)}, bf16[4,65536]{1,0:T(4,128)(2,1)S(1)}) %tuple.41), branch_computations={%region_6.7_spmd.clone, %region_7.11_spmd.clone} | conditional | flops 171017344 | bytes 22046800 | solution.py:60
  227.4 0.7 slice_reduce_fusion
  228.5 11.9 %copy.99 = bf16[16384,256]{1,0:T(8,128)(2,1)} copy(bf16[16384,256]{0,1:T(8,128)(2,1)} %get-tuple-element.208) | data formatting | bytes 16777216 | tf_op jit(solution)/shard_map
  240.3 1.3 fusion.95
  241.6 1.5 convolution_bitcast_fusion
  243.1 0.8 fusion.3
  244.6 0.8 fusion.81
  245.6 18.0 %conditional.5 = (f32[1,4,128]{2,1,0:T(4,128)}, f32[1,4,128,128]{3,2,1,0:T(8,128)S(1)}, f32[1,4,128]{2,1,0:T(4,128)S(1)}) conditional(s32[]{:T(128)} %convert_element_type.151, () %tuple.42, (s32[]{:T(128)}, s32[128]{0:T(128)S(1)}, s32[]{:T(128)}, bf16[16384,256]{0,1:T(8,128)(2,1)}, bf16[4,65536]{1,0:T(4,128)(2,1)S(1)}) %tuple.43), branch_computations={%region_12.13_spmd.clone, %region_13.17_spmd.clone} | conditional | flops 171017344 | bytes 22046800 | solution.py:60
  246.3 0.8 slice_reduce_fusion.1
  247.5 11.9 %copy.101 = bf16[16384,256]{1,0:T(8,128)(2,1)} copy(bf16[16384,256]{0,1:T(8,128)(2,1)} %get-tuple-element.219) | data formatting | bytes 16777216 | tf_op jit(solution)/shard_map
  259.3 1.3 fusion.96
  260.6 1.5 convolution_bitcast_fusion.1
  262.1 0.8 fusion.15
  263.6 0.8 fusion.82
  264.6 17.9 %conditional.6 = (f32[1,4,128]{2,1,0:T(4,128)}, f32[1,4,128,128]{3,2,1,0:T(8,128)S(1)}, f32[1,4,128]{2,1,0:T(4,128)S(1)}) conditional(s32[]{:T(128)} %convert_element_type.155, () %tuple.44, (s32[]{:T(128)}, s32[128]{0:T(128)S(1)}, s32[]{:T(128)}, bf16[16384,256]{0,1:T(8,128)(2,1)}, bf16[4,65536]{1,0:T(4,128)(2,1)S(1)}) %tuple.45), branch_computations={%region_18.19_spmd.clone, %region_19.23_spmd.clone} | conditional | flops 171017344 | bytes 22046800 | solution.py:60
  265.3 0.8 slice_reduce_fusion.2
  266.4 11.9 %copy.103 = bf16[16384,256]{1,0:T(8,128)(2,1)} copy(bf16[16384,256]{0,1:T(8,128)(2,1)} %get-tuple-element.230) | data formatting | bytes 16777216 | tf_op jit(solution)/shard_map
  278.3 1.3 fusion.97
  279.6 1.5 convolution_bitcast_fusion.2
  281.0 0.8 fusion.27
  282.5 0.8 fusion.83
  283.5 17.9 %conditional.7 = (f32[1,4,128]{2,1,0:T(4,128)}, f32[1,4,128,128]{3,2,1,0:T(8,128)S(1)}, f32[1,4,128]{2,1,0:T(4,128)S(1)}) conditional(s32[]{:T(128)} %convert_element_type.159, () %tuple.46, (s32[]{:T(128)}, s32[128]{0:T(128)S(1)}, s32[]{:T(128)}, bf16[16384,256]{0,1:T(8,128)(2,1)}, bf16[4,65536]{1,0:T(4,128)(2,1)S(1)}) %tuple.47), branch_computations={%region_24.25_spmd.clone, %region_25.29_spmd.clone} | conditional | flops 171017344 | bytes 22046800 | solution.py:60
  284.2 0.8 slice_reduce_fusion.3
  285.3 11.9 %copy.105 = bf16[16384,256]{1,0:T(8,128)(2,1)} copy(bf16[16384,256]{0,1:T(8,128)(2,1)} %get-tuple-element.241) | data formatting | bytes 16777216 | tf_op jit(solution)/shard_map
  297.2 1.3 fusion.98
  298.5 1.5 convolution_bitcast_fusion.3
  299.9 0.8 fusion.39
  301.5 0.8 fusion.84
  302.5 2.0 convolution_convert_fusion
  304.4 3.5 copy.108
  307.9 6.9 %all-to-all-start.2 = ((bf16[32,128,512]{2,1,0:T(8,128)(2,1)}), bf16[32,128,512]{2,1,0:T(8,128)(2,1)}, u32[]{:S(2)}, u32[]{:S(2)}) async-start(bf16[32,128,512]{2,1,0:T(8,128)(2,1)} %bitcast.168), calls=%async_computation.2 | async-start | bytes 8388608 | tf_op jit(solution)/shard_map/all_to_all | solution.py:157
  315.5 95.0 %all-to-all-done.2 = bf16[32,128,512]{2,1,0:T(8,128)(2,1)} async-done(((bf16[32,128,512]{2,1,0:T(8,128)(2,1)}), bf16[32,128,512]{2,1,0:T(8,128)(2,1)}, u32[]{:S(2)}, u32[]{:S(2)}) %all-to-all-start.2) | async-done | bytes 4194336 | tf_op jit(solution)/shard_map/all_to_all | solution.py:157
  410.5 4.6 %copy.109 = bf16[4,8,128,512]{3,1,2,0:T(8,128)(2,1)S(1)} copy(bf16[4,8,128,512]{3,2,1,0:T(8,128)(2,1)} %bitcast.93) | data formatting | bytes 8388608
  415.0 0.7 convolution_convert_fusion.2
  415.8 1.2 reshape.429
  (70 shorter events, 10.9 us)
Async XLA Ops:
  7.2 42.5 %copy-start = (bf16[4096,128]{1,0:T(8,128)(2,1)S(1)}, bf16[4096,128]{1,0:T(8,128)(2,1)}, u32[]{:S(2)}) copy-start(bf16[4096,128]{1,0:T(8,128)(2,1)} %param.19) | copy-start | bytes 3145732
  7.2 39.2 %all-gather.3.cloned.1.call-start = ((), (), s32[]{:S(2)}) async-start(), calls=%async_computation.3 | async-start | bytes 4718592 | tf_op jit(solution)/shard_map/all_gather | solution.py:86
  7.2 42.4 %copy-start.6 = (f32[4096]{0:T(1024)S(1)}, f32[4096]{0:T(1024)}, u32[]{:S(2)}) copy-start(f32[4096]{0:T(1024)} %param.16) | copy-start | bytes 49156
  7.9 218.8 %all-gather.5.cloned.1.call-start = ((), (), s32[]{:S(2)}) async-start(), calls=%async_computation.4 | async-start | bytes 8650752 | tf_op jit(solution)/shard_map/all_gather | solution.py:131
  46.4 3.4 copy-start.2
  49.8 1.5 copy-start.5
  51.4 2.3 copy-start.3
  54.5 21.1 %all-to-all-start = ((s32[32,1,1]{2,1,0:T(1,128)}), s32[32,1,1]{2,1,0:T(1,128)S(1)}, u32[]{:S(2)}, u32[]{:S(2)}) async-start(s32[32,1,1]{2,1,0:T(1,128)} %copy.83), calls=%async_computation | async-start | bytes 32768 | tf_op jit(solution)/shard_map/all_to_all | solution.py:115
  75.5 10.2 %copy-start.4 = (s32[128]{0:T(128)S(1)}, s32[128]{0:T(128)}, u32[]{:S(2)}) copy-start(s32[128]{0:T(128)} %param.20) | copy-start | bytes 1540
  75.5 125.2 %all-to-all-start.1 = ((bf16[32,128,512]{2,1,0:T(8,128)(2,1)}), bf16[32,128,512]{2,1,0:T(8,128)(2,1)}, u32[]{:S(2)}, u32[]{:S(2)}) async-start(bf16[32,128,512]{2,1,0:T(8,128)(2,1)} %bitcast.167), calls=%async_computation.1 | async-start | bytes 8388608 | tf_op jit(solution)/shard_map/all_to_all | solution.py:114
  307.9 102.6 %all-to-all-start.2 = ((bf16[32,128,512]{2,1,0:T(8,128)(2,1)}), bf16[32,128,512]{2,1,0:T(8,128)(2,1)}, u32[]{:S(2)}, u32[]{:S(2)}) async-start(bf16[32,128,512]{2,1,0:T(8,128)(2,1)} %bitcast.168), calls=%async_computation.2 | async-start | bytes 8388608 | tf_op jit(solution)/shard_map/all_to_all | solution.py:157
  415.0 2.0 copy-start.1
Sparse Core Ops, SparseCore 0:
  9.8 36.5 all-gather.2
  53.8 172.9 all-gather.4
where the time goes:
time: 426 us; the launch traced here: 424 us
  waiting for transfers between devices  262 us (62%)
  local copies, waits for them, and re-layouts  70.6 us (17%)
  starting transfers between devices  27.1 us (6%)
  matrix products  24.6 us (6%)
  between operations  19.4 us (5%)
  other arithmetic  17.4 us (4%)
    all_to_all x1, waiting for transfers between devices, shards(): lax.all_to_all(send_q, 'attn', split_axis=0, concat_axis=0, tiled=True)  107 us
    all_to_all x1, waiting for transfers between devices, shards(): lax.all_to_all(back, 'attn', split_axis=0, concat_axis=0, tiled=True)  95 us
    another operation x5, local copies, waits for them, and re-layouts  47.6 us
    all_gather x1, waiting for transfers between devices, shards(): lax.all_gather(tokens, 'proj', axis=1, tiled=True).astype(jnp.float32)  38.4 us
    all_gather x1, waiting for transfers between devices, shards(): piece = lax.all_gather(keys_values, 'attn', axis=0, tiled=True)  20.7 us
    unnamed x18, local copies, waits for them, and re-layouts  16.4 us
    all_to_all x1, starting transfers between devices, shards(): lax.all_to_all(send_q, 'attn', split_axis=0, concat_axis=0, tiled=True)  10.2 us
    all_to_all x1, starting transfers between devices, shards(): lax.all_to_all(send_id, 'attn', split_axis=0, concat_axis=0, tiled=True)  9.85 us
  transfers between devices with their start and end apart: 5, of which 4 were waited for; matrix products, arithmetic and copies ran while one was open for 5% of the time, Pallas kernels for 0%

commit v1 on v0

v1 whole, which is shorter than its diff:
```python
import jax
import jax.numpy as jnp
from jax import lax
from jax.sharding import PartitionSpec as P

HEAD = 128
QB = 128
NEG = -1e30
norm_eps = 1e-05


def shards(tokens, norm_gain, w_query, w_key, value_matrix, doc_lengths, block_server):
    rows = tokens.shape[0]
    model_width = w_query.shape[0]
    heads = w_query.shape[1] // HEAD
    blocks = rows // QB
    servers = lax.axis_size("attn")
    me = lax.axis_index("attn")
    wide = lax.all_gather(tokens, "proj", axis=1, tiled=True).astype(jnp.float32)
    scaled = (wide * norm_gain[None, :]).astype(jnp.bfloat16)
    squares = jnp.sum(wide * wide, axis=1, keepdims=True)
    inverse = lax.rsqrt(squares / model_width + norm_eps)
    dot = lambda w: (jnp.dot(scaled, w, preferred_element_type=jnp.float32) * inverse).astype(jnp.bfloat16)
    k = dot(w_key)
    v = dot(value_matrix)
    kv = jnp.concatenate([k, v], axis=1)
    prior = lax.ppermute(kv, "attn", [(i, (i + 1) % servers) for i in range(servers)])
    q = dot(w_query)
    allkv = jnp.concatenate([prior, kv], axis=0)
    starts = jnp.cumsum(doc_lengths) - doc_lengths
    extent = rows + QB
    outs, lses = [], []
    for b in range(blocks):
        pos = me * rows + b * QB + jnp.arange(QB, dtype=jnp.int32)
        first = jnp.max(jnp.where(starts[None, :] <= pos[:, None], starts[None, :], 0), axis=1)
        kpos = (me - 1) * rows + b * QB + jnp.arange(extent, dtype=jnp.int32)
        allowed = (kpos[None, :] >= first[:, None]) & (kpos[None, :] <= pos[:, None])
        win = allkv[b * QB:b * QB + extent]
        qb = q[b * QB:(b + 1) * QB].reshape(QB, heads, HEAD)
        s = jnp.einsum("qhd,kd->hqk", qb, win[:, :HEAD], preferred_element_type=jnp.float32)
        s = jnp.where(allowed, s * (1.0 / HEAD ** 0.5), NEG)
        m = jnp.max(s, axis=-1)
        w = jnp.where(allowed, jnp.exp(s - m[..., None]), 0.0)
        total = jnp.sum(w, axis=-1)
        o = jnp.einsum("hqk,kd->hqd", w.astype(jnp.bfloat16), win[:, HEAD:], preferred_element_type=jnp.float32)
        o = (o / total[..., None]).transpose(1, 0, 2).reshape(QB, heads * HEAD).astype(jnp.bfloat16)
        outs.append(o)
        lses.append(m + jnp.log(total))
    attn_out = jnp.concatenate(outs, axis=0)
    lse = jnp.stack(lses)
    slot = jnp.arange(servers, dtype=jnp.int32)
    sending = block_server[None, :] == slot[:, None]
    send = jnp.sum(jnp.where(sending[:, :, None, None], lse[None], 0.0), axis=1)
    flag = jnp.any(sending, axis=1).astype(jnp.float32)
    send = jnp.concatenate([send, jnp.broadcast_to(flag[:, None, None], (servers, 1, QB))], axis=1)
    recv = lax.all_to_all(send, "attn", split_axis=0, concat_axis=0, tiled=True)
    valid = recv[:, heads, 0] > 0
    rank = jnp.cumsum(valid.astype(jnp.int32)) - 1
    pick = (rank[None, :] == jnp.arange(blocks, dtype=jnp.int32)[:, None]) & valid[None, :]
    served = jnp.sum(jnp.where(pick[:, :, None, None], recv[None, :, :heads], 0.0), axis=1)
    return attn_out, served


def solution(mesh):
    return jax.shard_map(
        shards,
        mesh=mesh,
        in_specs=(
            P("attn", "proj"),
            P(),
            P(None, "proj"),
            P(None, "proj"),
            P(None, "proj"),
            P(),
            P("attn"),
        ),
        out_specs=(P("attn", "proj"), P("attn", "proj", None)),
        check_vma=False,
    )
```

time: 426 us -> 96.4 us (0.23)
  waiting for transfers between devices: 262 us -> 51.1 us
  local copies, waits for them, and re-layouts: 70.6 us -> 3.2 us
  starting transfers between devices: 27.1 us -> 8.99 us
  matrix products: 24.6 us -> 9.05 us
  other arithmetic: 17.4 us -> 9.3 us
  between operations: 19.4 us -> 14.4 us
    all_to_all x3 -> x1, waiting for transfers between devices: 202 us -> 7.14 us  [shards(): recv = lax.all_to_all(send, 'attn', split_axis=0, concat_axis=0, tiled=True)]
    another operation x5 -> x1, local copies, waits for them, and re-layouts: 47.6 us -> 0.76 us
    all_gather x1 -> x0, waiting for transfers between devices: 20.7 us -> none  [shards(): piece = lax.all_gather(keys_values, 'attn', axis=0, tiled=True)]
    all_to_all x3 -> x1, starting transfers between devices: 27 us -> 7.31 us  [shards(): recv = lax.all_to_all(send, 'attn', split_axis=0, concat_axis=0, tiled=True)]
    unnamed x18 -> x10, local copies, waits for them, and re-layouts: 16.4 us -> 0.22 us
    dot_general x15 -> x11, matrix products: 24.6 us -> 9.05 us  [the longest x3 5.48 us: shards(): jnp.dot(scaled, w, preferred_element_type=jnp.float32) * inverse]
    ppermute x0 -> x1, waiting for transfers between devices: none -> 8.1 us  [shards(): lax.ppermute(kv, 'attn', [(i, (i + 1) % servers) for i in range(servers)])]
  transfers between devices with their start and end apart: 5 -> 3, of which waited for: 4 -> 3; matrix products, arithmetic and copies ran while one was open for 5% -> 9% of each run, Pallas kernels for 0% -> 0%
where the time goes in v1:
time: 96.4 us; the launch traced here: 96 us
  waiting for transfers between devices  51.1 us (53%)
  between operations  14.4 us (15%)
  other arithmetic  9.3 us (10%)
  matrix products  9.05 us (9%)
  starting transfers between devices  8.99 us (9%)
  local copies, waits for them, and re-layouts  3.2 us (3%)
    all_gather x1, waiting for transfers between devices, shards(): lax.all_gather(tokens, 'proj', axis=1, tiled=True).astype(jnp.float32)  35.2 us
    ppermute x1, waiting for transfers between devices, shards(): lax.ppermute(kv, 'attn', [(i, (i + 1) % servers) for i in range(servers)])  8.1 us
    all_to_all x1, starting transfers between devices, shards(): recv = lax.all_to_all(send, 'attn', split_axis=0, concat_axis=0, tiled=True)  7.31 us
    all_to_all x1, waiting for transfers between devices, shards(): recv = lax.all_to_all(send, 'attn', split_axis=0, concat_axis=0, tiled=True)  7.14 us
    dot_general x3, matrix products, shards(): jnp.dot(scaled, w, preferred_element_type=jnp.float32) * inverse  5.48 us
    reduce_sum x1, other arithmetic, shards(): squares = jnp.sum(wide * wide, axis=1, keepdims=True)  3.23 us
    dot_general x4, matrix products, shards(): jnp.einsum('hqk,kd->hqd', w.astype(jnp.bfloat16), win[:, HEAD:], preferre...  2.09 us
  transfers between devices with their start and end apart: 3, of which 3 were waited for; matrix products, arithmetic and copies ran while one was open for 9% of the time, Pallas kernels for 0%

profile of v1, /device:TPU:2, one launch (start us, length us, event | category | flops | bytes accessed | tf_op | source)
XLA Modules:
  0.0 96.0 jit_solution(9389079406854169225)
XLA Ops:
  7.2 0.0 copy-start
  7.2 0.0 all-gather.2.cloned.1.call-start
  7.2 0.7 all-gather.2.cloned.1.call-update
  7.9 0.7 iota_compare_fusion.1
  8.7 0.8 copy.85
  9.4 0.2 reduce-window.17
  9.6 0.1 reduce
  9.7 0.7 sub.48
  10.5 0.2 select_reduce_fusion.5
  10.7 0.2 compare_and_fusion.2
  11.0 0.0 copy-start.4
  11.0 0.2 compare_and_fusion
  11.2 35.2 %all-gather.2.cloned.1.call-done = bf16[512,4096]{1,0:T(8,128)(2,1)} async-done(((bf16[512,512]{1,0:T(8,128)(2,1)}), bf16[512,4096]{1,0:T(8,128)(2,1)}) %all-gather.2.cloned.1.call-update) | async-done | bytes 4194320 | tf_op jit(solution)/shard_map/all_gather | solution.py:19
  46.4 3.2 %fusion.1 = f32[512]{0:T(512)S(1)} fusion(bf16[512,4096]{1,0:T(8,128)(2,1)} %all-gather.2.cloned.1.call-done), kind=kLoop, calls=%fused_computation.3 | loop fusion | flops 6290944 | bytes 4196352 | tf_op jit(solution)/shard_map/reduce_sum | solution.py:21
  49.6 0.2 copy-done.1
  49.8 1.5 %fusion.36 = bf16[512,128]{0,1:T(8,128)(2,1)S(1)} fusion(bf16[4096,128]{1,0:T(8,128)(2,1)S(1)} %copy-done, bf16[512,4096]{1,0:T(8,128)(2,1)S(1)} %copy-done.1, f32[4096]{0:T(1024)S(1)} %copy-done.4, f32[512]{0:T(512)S(1)} %add_rsqrt_fusion), kind=kOutput, calls=%fused_computation.39 | convolution fusion | flops 543293440 | bytes 5392384 | tf_op jit(solution)/shard_map/dot_general | solution.py:23
  51.4 1.5 %fusion.39 = bf16[512,128]{0,1:T(8,128)(2,1)S(1)} fusion(bf16[4096,128]{1,0:T(8,128)(2,1)S(1)} %copy-done.3, bf16[512,4096]{1,0:T(8,128)(2,1)S(1)} %copy-done.1, f32[4096]{0:T(1024)S(1)} %copy-done.4, f32[512]{0:T(512)S(1)} %add_rsqrt_fusion), kind=kOutput, calls=%fused_computation.40 | convolution fusion | flops 543293440 | bytes 5392384 | tf_op jit(solution)/shard_map/dot_general | solution.py:23
  52.9 1.6 %collective-permute-start = (bf16[512,256]{0,1:T(8,128)(2,1)S(1)}, bf16[512,256]{0,1:T(8,128)(2,1)S(1)}, u32[]{:S(2)}, u32[]{:S(2)}) collective-permute-start(bf16[512,256]{0,1:T(8,128)(2,1)S(1)} %pad_maximum_fusion.1), channel_id=1, source_target_pairs={{0,8},{8,16},{16,24},{24,32},{32,40},{40,48},{48,56},{56,64},{64,7... | collective-permute-start | bytes 786440 | tf_op jit(solution)/shard_map/ppermute | solution.py:27
  54.6 2.4 %fusion.19 = bf16[512,512]{0,1:T(8,128)(2,1)S(1)} fusion(bf16[4096,512]{1,0:T(8,128)(2,1)S(1)} %copy-done.2, bf16[512,4096]{1,0:T(8,128)(2,1)S(1)} %copy-done.1, f32[4096]{0:T(1024)S(1)} %copy-done.4, f32[512]{0:T(512)S(1)} %add_rsqrt_fusion), kind=kOutput, calls=%fused_computation.24 | convolution fusion | flops 2154299392 | bytes 8931328 | tf_op jit(solution)/shard_map/dot_general | solution.py:23
  57.0 0.1 fusion.72
  57.1 8.1 %collective-permute-done = bf16[512,256]{0,1:T(8,128)(2,1)S(1)} collective-permute-done((bf16[512,256]{0,1:T(8,128)(2,1)S(1)}, bf16[512,256]{0,1:T(8,128)(2,1)S(1)}, u32[]{:S(2)}, u32[]{:S(2)}) %collective-permute-start) | collective-permute-done | bytes 262176 | tf_op jit(solution)/shard_map/ppermute | solution.py:27
  65.2 0.1 maximum_maximum_fusion
  65.3 0.4 fusion.73
  65.7 0.3 fusion.48
  65.9 0.4 fusion.35
  66.3 0.4 fusion.74
  66.7 0.3 fusion.46
  66.9 0.4 fusion.34
  67.3 0.4 fusion.75
  67.7 0.3 fusion.44
  67.9 0.4 fusion.33
  68.3 0.4 fusion.76
  68.7 0.3 fusion.42
  69.0 0.1 select_reduce_fusion.1
  69.1 0.1 broadcast_in_dim.155
  69.1 0.7 copy.102
  69.8 7.3 %all-to-all-start = ((f32[32,5,128]{2,1,0:T(8,128)}), f32[32,5,128]{2,1,0:T(8,128)S(1)}, u32[]{:S(2)}, u32[]{:S(2)}) async-start(f32[32,5,128]{2,1,0:T(8,128)} %copy.102), calls=%async_computation | async-start | bytes 262144 | tf_op jit(solution)/shard_map/all_to_all | solution.py:56
  77.2 1.0 %fusion.32 = bf16[128,4,128]{0,2,1:T(8,128)(2,1)} fusion(f32[4,128,640]{1,2,0:T(8,128)S(1)} %get-tuple-element.21, f32[4,128]{1,0:T(4,128)S(1)} %get-tuple-element.20, pred[128,640]{0,1:T(8,128)(4,1)S(1)} %get-tuple-element.25, bf16[1024,256]{0,1:T(8,128)(2,1)S(1)} %maximum_maximum_fusion, f32[128,4]{0,1:T(4,128)S(1)} %bitcast.110), kind=kOutput, calls=%fused_computation.35 | convolution fusion | flops 85000192 | bytes 1691648 | tf_op jit(solution)/shard_map/hqk,kd->hqd/dot_general | solution.py:45
  78.2 0.1 copy.101
  78.3 0.1 copy.100
  78.4 0.1 copy.99
  78.5 1.0 %copy.98 = bf16[128,512]{1,0:T(8,128)(2,1)S(1)} copy(bf16[128,512]{0,1:T(8,128)(2,1)} %bitcast.104) | data formatting | bytes 262144 | tf_op jit(solution)/shard_map/convert_element_type | solution.py:46
  79.5 0.8 pad_maximum_fusion
  80.4 7.1 %all-to-all-done = f32[32,5,128]{2,1,0:T(8,128)S(1)} async-done(((f32[32,5,128]{2,1,0:T(8,128)}), f32[32,5,128]{2,1,0:T(8,128)S(1)}, u32[]{:S(2)}, u32[]{:S(2)}) %all-to-all-start) | async-done | bytes 81952 | tf_op jit(solution)/shard_map/all_to_all | solution.py:56
  87.5 0.7 compare_reduce_fusion
  88.2 0.1 reduce-window.18
  88.3 0.1 add_reduce_fusion
  88.4 0.7 select_reduce_fusion
  (27 shorter events, 0.2 us)
Async XLA Ops:
  7.2 42.5 %copy-start = (bf16[4096,128]{1,0:T(8,128)(2,1)S(1)}, bf16[4096,128]{1,0:T(8,128)(2,1)}, u32[]{:S(2)}) copy-start(bf16[4096,128]{1,0:T(8,128)(2,1)} %param.11) | copy-start | bytes 3145732
  7.2 39.2 %all-gather.2.cloned.1.call-start = ((), (), s32[]{:S(2)}) async-start(), calls=%async_computation.1 | async-start | bytes 4718592 | tf_op jit(solution)/shard_map/all_gather | solution.py:19
  11.0 38.7 %copy-start.4 = (f32[4096]{0:T(1024)S(1)}, f32[4096]{0:T(1024)}, u32[]{:S(2)}) copy-start(f32[4096]{0:T(1024)} %param.8) | copy-start | bytes 49156
  46.4 3.4 %copy-start.1 = (bf16[512,4096]{1,0:T(8,128)(2,1)S(1)}, bf16[512,4096]{1,0:T(8,128)(2,1)}, u32[]{:S(2)}) copy-start(bf16[512,4096]{1,0:T(8,128)(2,1)} %all-gather.2.cloned.1.call-done) | copy-start | bytes 12582916
  49.8 1.5 %copy-start.3 = (bf16[4096,128]{1,0:T(8,128)(2,1)S(1)}, bf16[4096,128]{1,0:T(8,128)(2,1)}, u32[]{:S(2)}) copy-start(bf16[4096,128]{1,0:T(8,128)(2,1)} %param.10) | copy-start | bytes 3145732
  51.4 3.2 %copy-start.2 = (bf16[4096,512]{1,0:T(8,128)(2,1)S(1)}, bf16[4096,512]{1,0:T(8,128)(2,1)}, u32[]{:S(2)}) copy-start(bf16[4096,512]{1,0:T(8,128)(2,1)} %param.9) | copy-start | bytes 12582916
  52.9 12.3 %collective-permute-start = (bf16[512,256]{0,1:T(8,128)(2,1)S(1)}, bf16[512,256]{0,1:T(8,128)(2,1)S(1)}, u32[]{:S(2)}, u32[]{:S(2)}) collective-permute-start(bf16[512,256]{0,1:T(8,128)(2,1)S(1)} %pad_maximum_fusion.1), channel_id=1, source_target_pairs={{0,8},{8,16},{16,24},{24,32},{32,40},{40,48},{48,56},{56,64},{64,7... | collective-permute-start | bytes 786440 | tf_op jit(solution)/shard_map/ppermute | solution.py:27
  69.8 17.7 %all-to-all-start = ((f32[32,5,128]{2,1,0:T(8,128)}), f32[32,5,128]{2,1,0:T(8,128)S(1)}, u32[]{:S(2)}, u32[]{:S(2)}) async-start(f32[32,5,128]{2,1,0:T(8,128)} %copy.102), calls=%async_computation | async-start | bytes 262144 | tf_op jit(solution)/shard_map/all_to_all | solution.py:56
Sparse Core Ops, SparseCore 0:
  9.8 36.5 all-gather.1

commit v2 on v1

v2 whole, which is shorter than its diff:
```python
import functools
import jax
import jax.numpy as jnp
from jax import lax
from jax.experimental import pallas as pl
from jax.experimental.pallas import tpu as pltpu
from jax.sharding import PartitionSpec as P

HEAD = 128
QB = 128
NEG = -1e30
EPS = 1e-05
LOG2E = 1.4426950408889634
LN2 = 0.6931471805599453
MESH = pl.DeviceIdType.MESH
NC = 4


def fused(n_attn, nz, tok, gain_h, wq, wk, wv, lens_h, served_h, out, lse_out,
          gain, lens, served, X, W, XS, G, KV, PKV, Q, FR, M, L, ACC, SLOT, RECV, PART,
          own_sem, in_sem, w_sem, s_sem, r_sem, kvs_sem, kvr_sem, ls_sem, lr_sem):
    f32 = jnp.float32
    bf16 = jnp.bfloat16
    a = lax.axis_index("attn")
    p = lax.axis_index("proj")
    core = lax.rem(p, 2)
    s = 1 - 2 * core
    mod8 = lambda v: lax.rem(v + 16, 8)
    partner = p + s
    ahead = mod8(p + 2 * s)
    behind = mod8(p - 2 * s)
    kinds = [p, partner, behind, ahead, mod8(p + 3 * s), mod8(p - s), mod8(p + 4), mod8(p + s + 4)]
    ny = n_attn // nz
    y = a // nz
    z = lax.rem(a, nz)
    offs = [(dy, dz) for dy in range(ny) for dz in range(nz) if (dy, dz) != (0, 0)]
    offs.sort(key=lambda o: -(min(o[0], ny - o[0]) + min(o[1], nz - o[1])))
    peers = [lax.rem(y + dy, ny) * nz + lax.rem(z + dz, nz) for dy, dz in offs]
    nxt = lax.rem(a + 1, n_attn)

    for t, k in enumerate(kinds):
        r = pl.ds(pl.multiple_of(k * 512, 512), 512)
        d = pl.ds(t * 512, 512)
        pltpu.make_async_copy(wq.at[r, :], W.at[d, pl.ds(0, 512)], w_sem.at[t, 0]).start()
        pltpu.make_async_copy(wk.at[r, :], W.at[d, pl.ds(512, 128)], w_sem.at[t, 1]).start()
        pltpu.make_async_copy(wv.at[r, :], W.at[d, pl.ds(640, 128)], w_sem.at[t, 2]).start()
    own_copy = pltpu.make_async_copy(tok, X.at[0], own_sem)
    own_copy.start()
    small = [pltpu.make_async_copy(src, dst, in_sem.at[i])
             for i, (src, dst) in enumerate(((gain_h, gain), (lens_h, lens), (served_h, served)))]
    for cp in small:
        cp.start()

    barrier = pltpu.get_barrier_semaphore()
    for d in (ahead, behind, partner):
        pl.semaphore_signal(barrier, inc=1, device_id=(a, d), device_id_type=MESH)
    for d in peers:
        pl.semaphore_signal(barrier, inc=1, device_id=(d, p), device_id_type=MESH)
    pl.semaphore_wait(barrier, 3 + len(peers))

    def rows(c):
        return pl.ds((NC - 1 - c) * QB, QB)

    def rc(c, kind, src, dst_proj):
        return pltpu.make_async_remote_copy(
            src_ref=src, dst_ref=X.at[kind, rows(c), :],
            send_sem=s_sem.at[c, kind], recv_sem=r_sem.at[c, kind],
            device_id=(a, dst_proj), device_id_type=MESH)

    def send_own(c):
        src = tok.at[rows(c), :]
        rc(c, 2, src, ahead).start()
        rc(c, 3, src, behind).start()
        rc(c, 1, src, partner).start()

    def recv(c, kind):
        rc(c, kind, X.at[kind, rows(c), :], partner).wait_recv()

    def relay_near(c):
        recv(c, 2)
        rc(c, 6, X.at[2, rows(c), :], ahead).start()
        rc(c, 4, X.at[2, rows(c), :], partner).start()
        recv(c, 3)
        rc(c, 5, X.at[3, rows(c), :], partner).start()

    def relay_far(c):
        recv(c, 6)
        rc(c, 7, X.at[6, rows(c), :], partner).start()

    def recv_partner(c):
        for k in (1, 4, 5, 7):
            recv(c, k)

    send_own(0)
    send_own(1)

    for cp in small:
        cp.wait()
    lane = lax.broadcasted_iota(jnp.int32, (8, 128), 1)
    ln = jnp.broadcast_to(lens[...].astype(f32), (8, 128))
    cum = ln
    for k in (1, 2, 4, 8, 16, 32, 64):
        cum = cum + jnp.where(lane >= k, pltpu.roll(cum, k, 1), 0.0)
    starts = (cum - ln)[0:1, :]
    base = (a * (NC * QB)).astype(f32)
    sub = lax.broadcasted_iota(jnp.int32, (QB, QB), 0).astype(f32)
    for i in range(NC):
        pos = sub + (base + float(QB * i))
        cand = jnp.where(starts <= pos, jnp.broadcast_to(starts, (QB, QB)), 0.0)
        first = jnp.max(cand, axis=1, keepdims=True) - base
        FR[i] = jnp.broadcast_to(first, (QB, QB))
    for t, k in enumerate(kinds):
        for u in range(4):
            G[t, 0:1, u * 128:(u + 1) * 128] = gain[pl.ds(4 * k + u, 1), :]

    def kv_copy(j):
        return pltpu.make_async_remote_copy(
            src_ref=KV.at[j], dst_ref=PKV.at[j], send_sem=kvs_sem.at[j], recv_sem=kvr_sem.at[j],
            device_id=(nxt, p), device_id_type=MESH)

    def scale(j, ks, sq):
        for t in ks:
            xf = X[t, j * QB:(j + 1) * QB, :].astype(f32)
            XS[:, t * 512:(t + 1) * 512] = (xf * G[t, 0:1, :]).astype(bf16)
            x2 = xf * xf
            part = (x2[:, 0:128] + x2[:, 128:256]) + (x2[:, 256:384] + x2[:, 384:512])
            sq = part if sq is None else sq + part
        return sq

    def project(j, acc, sq):
        inv = lax.rsqrt(jnp.sum(sq, axis=1, keepdims=True) * (1.0 / 4096) + EPS)
        KV[j, :, :] = (acc[:, 512:768] * inv).astype(bf16)
        kv_copy(j).start()
        for h in range(4):
            Q[j, h * QB:(h + 1) * QB, :] = (acc[:, h * 128:(h + 1) * 128] * inv).astype(bf16)

    lane_f = lax.broadcasted_iota(jnp.int32, (QB, QB), 1).astype(f32)

    def update(i, parts, init):
        cs = LOG2E / HEAD ** 0.5
        masks = []
        for own, j in parts:
            off = float(QB * j - (0 if own else NC * QB))
            ok = (lane_f + off) >= FR[i]
            if own and j == i:
                ok = ok & (lane_f <= sub)
            masks.append(ok)
        for h in range(4):
            hr = slice(h * QB, (h + 1) * QB)
            q = Q[i, hr, :]
            ss = []
            for (own, j), ok in zip(parts, masks):
                kk = (KV if own else PKV)[j, :, 0:128]
                sc = lax.dot_general(q, kk, (((1,), (1,)), ((), ())), preferred_element_type=f32) * cs
                ss.append(jnp.where(ok, sc, NEG))
            mx = functools.reduce(jnp.maximum, ss)
            mx = jnp.broadcast_to(jnp.max(mx, axis=1, keepdims=True), (QB, QB))
            if not init:
                mo = M[i, hr, :]
                mx = jnp.maximum(mx, mo)
            ps = [jnp.exp2(sc - mx) for sc in ss]
            tot = functools.reduce(jnp.add, ps)
            tot = jnp.broadcast_to(jnp.sum(tot, axis=1, keepdims=True), (QB, QB))
            o = None
            for (own, j), pp in zip(parts, ps):
                vv = (KV if own else PKV)[j, :, 128:256]
                d = jnp.dot(pp.astype(bf16), vv, preferred_element_type=f32)
                o = d if o is None else o + d
            if not init:
                al = jnp.exp2(mo - mx)
                tot = tot + al * L[i, hr, :]
                o = o + al * ACC[i, hr, :]
            M[i, hr, :] = mx
            L[i, hr, :] = tot
            ACC[i, hr, :] = o

    def attend(j):
        for i in range(NC - 1, j + 1, -1):
            update(i, [(True, j)], False)
        if j + 1 < NC:
            kv_copy(j + 1).wait_recv()
            update(j + 1, [(True, j), (False, j + 1)], False)
        update(j, [(True, j)] + [(False, k) for k in range(j + 1, NC)], True)

    relay_near(0)
    send_own(2)
    relay_near(1)
    send_own(3)
    own_copy.wait()
    for t, k in enumerate(kinds):
        r = pl.ds(pl.multiple_of(k * 512, 512), 512)
        d = pl.ds(t * 512, 512)
        pltpu.make_async_copy(wq.at[r, :], W.at[d, pl.ds(0, 512)], w_sem.at[t, 0]).wait()
        pltpu.make_async_copy(wk.at[r, :], W.at[d, pl.ds(512, 128)], w_sem.at[t, 1]).wait()
        pltpu.make_async_copy(wv.at[r, :], W.at[d, pl.ds(640, 128)], w_sem.at[t, 2]).wait()

    for c in range(NC - 1):
        j = NC - 1 - c
        relay_far(c)
        recv_partner(c)
        sq = scale(j, range(8), None)
        acc = jnp.dot(XS[...], W[...], preferred_element_type=f32)
        project(j, acc, sq)
        if c + 2 < NC:
            relay_near(c + 2)
        attend(j)

    c = NC - 1
    for k in (1, 4, 5):
        recv(c, k)
    sq = scale(0, range(6), None)
    PART[...] = jnp.dot(XS[:, :3072], W[:3072, :], preferred_element_type=f32)
    relay_far(c)
    sq = scale(0, (6,), sq)
    recv(c, 7)
    sq = scale(0, (7,), sq)
    acc = PART[...] + jnp.dot(XS[:, 3072:], W[3072:, :], preferred_element_type=f32)
    project(0, acc, sq)
    attend(0)
    kv_copy(0).wait_recv()
    update(0, [(False, 0)], False)

    eye = sub == lane_f
    tiles = []
    srow = lax.broadcasted_iota(jnp.int32, (8, 128), 0)
    for i in range(NC):
        tile = jnp.ones((8, 128), f32)
        for h in range(4):
            hr = slice(h * QB, (h + 1) * QB)
            v = (M[i, hr, :] + jnp.log2(L[i, hr, :])) * LN2
            row = jnp.sum(jnp.where(eye, v, 0.0), axis=0, keepdims=True)
            tile = jnp.where(srow == h, jnp.broadcast_to(row, (8, 128)), tile)
        tiles.append(tile)
    srv = [served[i] for i in range(NC)]
    for d in range(n_attn):
        t = jnp.where(srv[0] == d, tiles[0], 0.0)
        for i in range(1, NC):
            t = t + jnp.where(srv[i] == d, tiles[i], 0.0)
        SLOT[d] = t

    def lse_copy(dst, slot):
        return pltpu.make_async_remote_copy(
            src_ref=SLOT.at[dst], dst_ref=RECV.at[slot], send_sem=ls_sem.at[dst], recv_sem=lr_sem.at[slot],
            device_id=(dst, p), device_id_type=MESH)

    for d in peers:
        lse_copy(d, a).start()
    RECV[a] = SLOT[a]

    for i in range(NC):
        for h in range(4):
            hr = slice(h * QB, (h + 1) * QB)
            out[i * QB:(i + 1) * QB, h * 128:(h + 1) * 128] = (ACC[i, hr, :] / L[i, hr, :]).astype(bf16)

    for d in peers:
        lse_copy(d, d).wait_recv()
    cnt = jnp.zeros((4, 128), f32)
    res = [jnp.zeros((4, 128), f32) for _ in range(NC)]
    for d in range(n_attn):
        t = RECV[d]
        f = jnp.broadcast_to(t[4:5, :], (4, 128))
        for i in range(NC):
            res[i] = jnp.where((cnt == float(i)) & (f > 0.5), t[0:4, :], res[i])
        cnt = cnt + f
    for i in range(NC):
        lse_out[i] = res[i]

    for c in range(NC):
        for k in (1, 2, 3, 4, 5, 6, 7):
            rc(c, k, X.at[k, rows(c), :], partner).wait_send()
    for j in range(NC):
        kv_copy(j).wait_send()
    for d in peers:
        lse_copy(d, a).wait_send()


def shards(n_attn, nz, tokens, norm_gain, w_query, w_key, value_matrix, doc_lengths, block_server):
    hbm = pl.BlockSpec(memory_space=pltpu.HBM)
    vm = pl.BlockSpec(memory_space=pltpu.VMEM)
    bf16, f32 = jnp.bfloat16, jnp.float32
    dma = pltpu.SemaphoreType.DMA
    return pl.pallas_call(
        functools.partial(fused, n_attn, nz),
        out_shape=(jax.ShapeDtypeStruct((512, 512), bf16), jax.ShapeDtypeStruct((4, 4, 128), f32)),
        in_specs=[hbm] * 7,
        out_specs=(vm, vm),
        scratch_shapes=[
            pltpu.VMEM((32, 128), f32),
            pltpu.VMEM((1, 128), jnp.int32),
            pltpu.SMEM((4,), jnp.int32),
            pltpu.VMEM((8, 512, 512), bf16),
            pltpu.VMEM((4096, 768), bf16),
            pltpu.VMEM((QB, 4096), bf16),
            pltpu.VMEM((8, 1, 512), f32),
            pltpu.VMEM((NC, QB, 256), bf16),
            pltpu.VMEM((NC, QB, 256), bf16),
            pltpu.VMEM((NC, 4 * QB, 128), bf16),
            pltpu.VMEM((NC, QB, QB), f32),
            pltpu.VMEM((NC, 4 * QB, 128), f32),
            pltpu.VMEM((NC, 4 * QB, 128), f32),
            pltpu.VMEM((NC, 4 * QB, 128), f32),
            pltpu.VMEM((n_attn, 8, 128), f32),
            pltpu.VMEM((n_attn, 8, 128), f32),
            pltpu.VMEM((QB, 768), f32),
            dma(()), dma((3,)), dma((8, 3)), dma((NC, 8)), dma((NC, 8)), dma((NC,)), dma((NC,)),
            dma((n_attn,)), dma((n_attn,)),
        ],
        compiler_params=pltpu.CompilerParams(
            collective_id=0, has_side_effects=True, vmem_limit_bytes=67043328),
        name="fused_attention",
    )(tokens, norm_gain.reshape(32, 128), w_query, w_key, value_matrix,
      doc_lengths.reshape(1, 128), block_server)


def solution(mesh):
    n_attn = mesh.shape["attn"]
    nz = 8 if n_attn % 8 == 0 else n_attn
    return jax.shard_map(
        functools.partial(shards, n_attn, nz),
        mesh=mesh,
        in_specs=(
            P("attn", "proj"),
            P(),
            P(None, "proj"),
            P(None, "proj"),
            P(None, "proj"),
            P(),
            P("attn"),
        ),
        out_specs=(P("attn", "proj"), P("attn", "proj", None)),
        check_vma=False,
    )
```

time: 96.4 us -> 56.7 us (0.59)
  the two profiles are of different devices: /device:TPU:2 before, /device:TPU:1 now
where the time goes in v2:
time: 56.7 us; the launch traced here: 56.5 us
  Pallas kernels  52.7 us (93%)
  local copies, waits for them, and re-layouts  3.16 us (6%)
  between operations  0.64 us (1%)
    pallas_call x1, Pallas kernels, shards(): pl.pallas_call(functools.partial(fused, n_attn, nz), out_shape=(jax.Shape...  52.7 us
    unnamed x2, local copies, waits for them, and re-layouts  3.16 us

profile of v2, /device:TPU:1, one launch (start us, length us, event | category | flops | bytes accessed | tf_op | source)
XLA Modules:
  0.0 56.5 jit_solution(2710979939287045940)
XLA Ops:
  0.6 52.7 %fused_attention.1 = (bf16[512,512]{1,0:T(8,128)(2,1)}, f32[4,4,128]{2,1,0:T(4,128)}) custom-call(bf16[512,512]{1,0:T(8,128)(2,1)} %tok.1, f32[32,128]{1,0:T(8,128)} %bitcast.2, bf16[4096,512]{1,0:T(8,128)(2,1)} %wq.1, bf16[4096,128]{1,0:T(8,128)(2,1)} %wk.1, bf16[4096,128]{1,0:T(8,128)(2,1)} %wv.1, s32[1,128]{1,0:T(1,128)} %bitcast.3, s32[4]{0:T(128)} %served_h.1), custom_call_target="tpu_custom_call" | custom-call | tf_op jit(solution)/shard_map/fused_attention/pallas_call | solution.py:282
  53.4 1.9 %copy.11 = bf16[512,512]{1,0:T(8,128)(2,1)} copy(bf16[512,512]{1,0:T(8,128)(2,1)} %get-tuple-element.4) | data formatting | bytes 1048576
  55.2 1.3 %copy.12 = f32[4,4,128]{2,1,0:T(4,128)} copy(f32[4,4,128]{2,1,0:T(4,128)} %get-tuple-element.5) | data formatting | bytes 16384

commit v3 on v2

v3 whole, which is shorter than its diff:
```python
import functools
import jax
import jax.numpy as jnp
from jax import lax
from jax.experimental import pallas as pl
from jax.experimental.pallas import tpu as pltpu
from jax.sharding import PartitionSpec as P

HEAD = 128
QB = 128
NEG = -1e30
EPS = 1e-05
LOG2E = 1.4426950408889634
LN2 = 0.6931471805599453
MESH = pl.DeviceIdType.MESH
NC = 4


def fused(n_attn, nz, tok, gain_h, wq, wk, wv, lens_h, served_h, out, lse_out,
          gain, lens, served, TOK, X, W, SQ, PSQ, INV, KV, PKV, Q, FR, M, L, ACC, LT, SLOT, RECV, PART,
          in_sem, w_sem, s_sem, r_sem, kvs_sem, kvr_sem, ls_sem, lr_sem, hop_sem):
    f32 = jnp.float32
    bf16 = jnp.bfloat16
    a = lax.axis_index("attn")
    p = lax.axis_index("proj")
    core = lax.rem(p, 2)
    s = 1 - 2 * core
    mod8 = lambda v: lax.rem(v + 16, 8)
    partner = p + s
    ahead = mod8(p + 2 * s)
    behind = mod8(p - 2 * s)
    kinds = [p, partner, behind, ahead, mod8(p + 3 * s), mod8(p - s), mod8(p + 4), mod8(p + s + 4)]
    ny = n_attn // nz
    y = a // nz
    z = lax.rem(a, nz)
    at = lambda dy, dz: lax.rem(y + dy, ny) * nz + lax.rem(z + dz, nz)
    offs = [(dy, dz) for dy in range(ny) for dz in range(nz) if (dy, dz) != (0, 0)]
    offs.sort(key=lambda o: -(min(o[0], ny - o[0]) + min(o[1], nz - o[1])))
    peers = [at(dy, dz) for dy, dz in offs]
    zs = (at(0, 1), at(0, nz - 1))
    ys = (at(1, 0), at(ny - 1, 0))
    nxt = lax.rem(a + 1, n_attn)
    prv = lax.rem(a + n_attn - 1, n_attn)

    small = [pltpu.make_async_copy(src, dst, in_sem.at[i])
             for i, (src, dst) in enumerate(((tok, TOK), (gain_h, gain), (lens_h, lens), (served_h, served)))]
    for cp in small:
        cp.start()

    barrier = pltpu.get_barrier_semaphore()
    for d in (ahead, behind, partner):
        pl.semaphore_signal(barrier, inc=1, device_id=(a, d), device_id_type=MESH)
    for d in zs + ys + (nxt, prv):
        pl.semaphore_signal(barrier, inc=1, device_id=(d, p), device_id_type=MESH)

    def w_copies(t, k):
        r = pl.ds(pl.multiple_of(k * 512, 512), 512)
        d = pl.ds(t * 512, 512)
        return (pltpu.make_async_copy(wq.at[r, :], W.at[d, pl.ds(0, 512)], w_sem.at[t, 0]),
                pltpu.make_async_copy(wk.at[r, :], W.at[d, pl.ds(512, 128)], w_sem.at[t, 1]),
                pltpu.make_async_copy(wv.at[r, :], W.at[d, pl.ds(640, 128)], w_sem.at[t, 2]))

    for t, k in enumerate(kinds):
        for cp in w_copies(t, k):
            cp.start()
    for cp in small:
        cp.wait()

    lane = lax.broadcasted_iota(jnp.int32, (QB, QB), 1).astype(f32)
    sub = lax.broadcasted_iota(jnp.int32, (QB, QB), 0).astype(f32)
    eye = sub == lane

    g = jnp.concatenate([gain[pl.ds(4 * p + u, 1), :] for u in range(4)], axis=1)

    def scale_rows(n, carry):
        r = pl.ds(pl.multiple_of(n * 32, 32), 32)
        xf = TOK[r, :].astype(f32)
        X[0, r, :] = (xf * g).astype(bf16)
        x2 = xf * xf
        PSQ[r, :] = (x2[:, 0:128] + x2[:, 128:256]) + (x2[:, 256:384] + x2[:, 384:512])
        return carry

    lax.fori_loop(0, NC * QB // 32, scale_rows, 0)
    for j in range(NC):
        col = jnp.sum(PSQ[j * QB:(j + 1) * QB, :], axis=1, keepdims=True)
        SQ[0, j:j + 1, :] = jnp.sum(jnp.where(eye, col, 0.0), axis=0, keepdims=True)
        SQ[0, NC + j:NC + j + 1, :] = jnp.zeros((1, QB), f32)

    pl.semaphore_wait(barrier, 9)

    def hop_signal(k):
        for d in (zs if k < 3 else ys):
            pl.semaphore_signal(hop_sem.at[k], inc=1, device_id=(d, p), device_id_type=MESH)

    def hop(k):
        pl.semaphore_wait(hop_sem.at[k], 2)
        if k < 4:
            hop_signal(k + 1)

    hop_signal(0)

    def view(c, kind):
        if c == NC:
            return SQ.at[kind]
        return X.at[kind, pl.ds((NC - 1 - c) * QB, QB), :]

    def rc(c, kind, src_kind, dst_proj):
        return pltpu.make_async_remote_copy(
            src_ref=view(c, src_kind), dst_ref=view(c, kind),
            send_sem=s_sem.at[c, kind], recv_sem=r_sem.at[c, kind],
            device_id=(a, dst_proj), device_id_type=MESH)

    def send_own(c):
        rc(c, 2, 0, ahead).start()
        rc(c, 3, 0, behind).start()
        rc(c, 1, 0, partner).start()

    def recv(c, kind):
        rc(c, kind, kind, partner).wait_recv()

    def relay_near(c):
        recv(c, 2)
        rc(c, 6, 2, ahead).start()
        rc(c, 4, 2, partner).start()
        recv(c, 3)
        rc(c, 5, 3, partner).start()

    def relay_far(c):
        recv(c, 6)
        rc(c, 7, 6, partner).start()

    def recv_partner(c):
        for k in (1, 4, 5, 7):
            recv(c, k)

    send_own(NC)
    send_own(0)
    send_own(1)

    ln = jnp.broadcast_to(lens[...].astype(f32), (8, 128))
    cum = ln
    for k in (1, 2, 4, 8, 16, 32, 64):
        cum = cum + jnp.where(lane[0:8] >= k, pltpu.roll(cum, k, 1), 0.0)
    starts = jnp.sum(jnp.where(eye, (cum - ln)[0:1, :], 0.0), axis=1, keepdims=True)
    base = (a * (NC * QB)).astype(f32)
    for i in range(NC):
        pos = lane + (base + float(QB * i))
        first = jnp.max(jnp.where(starts <= pos, starts, 0.0), axis=0, keepdims=True)
        FR[i:i + 1, :] = first - base

    def kv_copy(j):
        return pltpu.make_async_remote_copy(
            src_ref=KV.at[j], dst_ref=PKV.at[j], send_sem=kvs_sem.at[j], recv_sem=kvr_sem.at[j],
            device_id=(nxt, p), device_id_type=MESH)

    def lhs(j, ks):
        return jnp.concatenate([X[t, j * QB:(j + 1) * QB, :] for t in ks], axis=1)

    def project(j, acc):
        inv = INV[j]
        KV[j, 0] = (acc[:, 512:640] * inv).astype(bf16)
        KV[j, 1] = jnp.transpose(acc[:, 640:768] * inv).astype(bf16)
        kv_copy(j).start()
        for h in range(4):
            Q[j, h * QB:(h + 1) * QB, :] = (acc[:, h * 128:(h + 1) * 128] * inv).astype(bf16)

    def update(i, parts, init):
        cs = LOG2E / HEAD ** 0.5
        n = len(parts)
        oks = []
        for own, j in parts:
            off = float(QB * j - (0 if own else NC * QB))
            ok = (sub + off) >= FR[i:i + 1, :]
            if own and j == i:
                ok = ok & (sub <= lane)
            oks.append(ok)
        bufs = [(KV if own else PKV).at[j] for own, j in parts]
        kk = jnp.concatenate([b[0] for b in bufs], axis=0)
        vv = jnp.concatenate([b[1] for b in bufs], axis=1)
        for hp in range(2):
            q = Q[i, hp * 256:(hp + 1) * 256, :]
            sc = lax.dot_general(kk, q, (((1,), (1,)), ((), ())), preferred_element_type=f32)
            halves, als = [], []
            for u in range(2):
                h = 2 * hp + u
                ss = [jnp.where(oks[t], sc[t * QB:(t + 1) * QB, u * 128:(u + 1) * 128] * cs, NEG) for t in range(n)]
                mx = jnp.max(functools.reduce(jnp.maximum, ss), axis=0, keepdims=True)
                if not init:
                    mo = M[i, h:h + 1, :]
                    mx = jnp.maximum(mx, mo)
                ps = [jnp.exp2(x - mx) for x in ss]
                tot = jnp.sum(functools.reduce(jnp.add, ps), axis=0, keepdims=True)
                if not init:
                    al = jnp.exp2(mo - mx)
                    als.append(al)
                    tot = tot + al * L[i, h:h + 1, :]
                M[i, h:h + 1, :] = mx
                L[i, h:h + 1, :] = tot
                halves.append(jnp.concatenate([x.astype(bf16) for x in ps], axis=0))
            o = jnp.dot(vv, jnp.concatenate(halves, axis=1), preferred_element_type=f32)
            cols = slice(hp * 256, (hp + 1) * 256)
            if not init:
                o = o + jnp.concatenate(als, axis=1) * ACC[i, :, cols]
            ACC[i, :, cols] = o

    def attend(j):
        for i in range(NC - 1, j + 1, -1):
            update(i, [(True, j)], False)
        if j + 1 < NC:
            kv_copy(j + 1).wait_recv()
            update(j + 1, [(True, j), (False, j + 1)], False)
        parts = [(True, j)] + [(False, k) for k in range(NC - 1, j, -1)]
        for t in range(0, len(parts), 2):
            update(j, parts[t:t + 2], t == 0)

    relay_near(NC)
    relay_near(0)
    send_own(2)
    hop(0)
    relay_far(NC)
    relay_near(1)
    send_own(3)
    hop(1)
    recv_partner(NC)
    tot = SQ[0]
    for t in range(1, 8):
        tot = tot + SQ[t]
    rows_inv = lax.rsqrt(tot * (1.0 / 4096) + EPS)
    for j in range(NC):
        INV[j] = jnp.broadcast_to(jnp.sum(jnp.where(eye, rows_inv[j:j + 1, :], 0.0), axis=1, keepdims=True), (QB, QB))
    for t, k in enumerate(kinds):
        for cp in w_copies(t, k):
            cp.wait()

    for c in range(NC - 1):
        j = NC - 1 - c
        relay_far(c)
        hop(c + 2)
        recv_partner(c)
        acc = jnp.dot(lhs(j, range(8)), W[...], preferred_element_type=f32)
        project(j, acc)
        if c + 2 < NC:
            relay_near(c + 2)
        attend(j)

    c = NC - 1
    for k in (1, 4, 5):
        recv(c, k)
    PART[...] = jnp.dot(lhs(0, range(6)), W[:3072, :], preferred_element_type=f32)
    relay_far(c)
    recv(c, 7)
    project(0, PART[...] + jnp.dot(lhs(0, (6, 7)), W[3072:, :], preferred_element_type=f32))
    attend(0)
    kv_copy(0).wait_recv()
    update(0, [(False, 0)], False)

    for i in range(NC):
        LT[i, 0:4, :] = (M[i] + jnp.log2(L[i])) * LN2
        LT[i, 4:8, :] = jnp.ones((4, 128), f32)
    tiles = [LT[i] for i in range(NC)]
    srv = [served[i] for i in range(NC)]
    for d in range(n_attn):
        t = jnp.where(srv[0] == d, tiles[0], 0.0)
        for i in range(1, NC):
            t = t + jnp.where(srv[i] == d, tiles[i], 0.0)
        SLOT[d] = t

    def lse_copy(dst, slot):
        return pltpu.make_async_remote_copy(
            src_ref=SLOT.at[dst], dst_ref=RECV.at[slot], send_sem=ls_sem.at[dst], recv_sem=lr_sem.at[slot],
            device_id=(dst, p), device_id_type=MESH)

    for d in peers:
        lse_copy(d, a).start()
    RECV[a] = SLOT[a]

    for i in range(NC):
        for h in range(4):
            o = ACC[i, :, h * 128:(h + 1) * 128] / L[i, h:h + 1, :]
            out[i * QB:(i + 1) * QB, h * 128:(h + 1) * 128] = jnp.transpose(o).astype(bf16)

    for d in peers:
        lse_copy(d, d).wait_recv()
    cnt = jnp.zeros((4, 128), f32)
    res = [jnp.zeros((4, 128), f32) for _ in range(NC)]
    for d in range(n_attn):
        t = RECV[d]
        f = jnp.broadcast_to(t[4:5, :], (4, 128))
        for i in range(NC):
            res[i] = jnp.where((cnt == float(i)) & (f > 0.5), t[0:4, :], res[i])
        cnt = cnt + f
    for i in range(NC):
        lse_out[i] = res[i]

    for c in range(NC + 1):
        for k in (1, 2, 3, 4, 5, 6, 7):
            rc(c, k, k, partner).wait_send()
    for j in range(NC):
        kv_copy(j).wait_send()
    for d in peers:
        lse_copy(d, a).wait_send()


def shards(n_attn, nz, tokens, norm_gain, w_query, w_key, value_matrix, doc_lengths, block_server):
    hbm = pl.BlockSpec(memory_space=pltpu.HBM)
    vm = pl.BlockSpec(memory_space=pltpu.VMEM)
    bf16, f32 = jnp.bfloat16, jnp.float32
    dma = pltpu.SemaphoreType.DMA
    return pl.pallas_call(
        functools.partial(fused, n_attn, nz),
        out_shape=(jax.ShapeDtypeStruct((512, 512), bf16), jax.ShapeDtypeStruct((4, 4, 128), f32)),
        in_specs=[hbm] * 7,
        out_specs=(vm, vm),
        scratch_shapes=[
            pltpu.VMEM((32, 128), f32),
            pltpu.VMEM((1, 128), jnp.int32),
            pltpu.SMEM((4,), jnp.int32),
            pltpu.VMEM((512, 512), bf16),
            pltpu.VMEM((8, 512, 512), bf16),
            pltpu.VMEM((4096, 768), bf16),
            pltpu.VMEM((8, 8, 128), f32),
            pltpu.VMEM((512, 128), f32),
            pltpu.VMEM((NC, QB, QB), f32),
            pltpu.VMEM((NC, 2, QB, 128), bf16),
            pltpu.VMEM((NC, 2, QB, 128), bf16),
            pltpu.VMEM((NC, 4 * QB, 128), bf16),
            pltpu.VMEM((8, QB), f32),
            pltpu.VMEM((NC, 4, 128), f32),
            pltpu.VMEM((NC, 4, 128), f32),
            pltpu.VMEM((NC, 128, 4 * QB), f32),
            pltpu.VMEM((NC, 8, 128), f32),
            pltpu.VMEM((n_attn, 8, 128), f32),
            pltpu.VMEM((n_attn, 8, 128), f32),
            pltpu.VMEM((QB, 768), f32),
            dma((4,)), dma((8, 3)), dma((NC + 1, 8)), dma((NC + 1, 8)), dma((NC,)), dma((NC,)),
            dma((n_attn,)), dma((n_attn,)), pltpu.SemaphoreType.REGULAR((5,)),
        ],
        compiler_params=pltpu.CompilerParams(
            collective_id=0, has_side_effects=True, vmem_limit_bytes=67043328),
        name="fused_attention",
    )(tokens, norm_gain.reshape(32, 128), w_query, w_key, value_matrix,
      doc_lengths.reshape(1, 128), block_server)


def solution(mesh):
    n_attn = mesh.shape["attn"]
    nz = 8 if n_attn % 8 == 0 else n_attn
    return jax.shard_map(
        functools.partial(shards, n_attn, nz),
        mesh=mesh,
        in_specs=(
            P("attn", "proj"),
            P(),
            P(None, "proj"),
            P(None, "proj"),
            P(None, "proj"),
            P(),
            P("attn"),
        ),
        out_specs=(P("attn", "proj"), P("attn", "proj", None)),
        check_vma=False,
    )
```

time: 56.7 us -> 50.6 us (0.89)
  the two profiles are of different devices: /device:TPU:1 before, /device:TPU:2 now
where the time goes in v3:
time: 50.6 us; the launch traced here: 49.7 us
  Pallas kernels  45.9 us (91%)
  local copies, waits for them, and re-layouts  3.16 us (6%)
  between operations  0.64 us (1%)
    pallas_call x1, Pallas kernels, shards(): pl.pallas_call(functools.partial(fused, n_attn, nz), out_shape=(jax.Shape...  45.9 us
    unnamed x2, local copies, waits for them, and re-layouts  3.16 us

profile of v3, /device:TPU:2, one launch (start us, length us, event | category | flops | bytes accessed | tf_op | source)
XLA Modules:
  0.0 49.7 jit_solution(13690906314191937868)
XLA Ops:
  0.6 45.9 %fused_attention.1 = (bf16[512,512]{1,0:T(8,128)(2,1)}, f32[4,4,128]{2,1,0:T(4,128)}) custom-call(bf16[512,512]{1,0:T(8,128)(2,1)} %tok.1, f32[32,128]{1,0:T(8,128)} %bitcast.2, bf16[4096,512]{1,0:T(8,128)(2,1)} %wq.1, bf16[4096,128]{1,0:T(8,128)(2,1)} %wk.1, bf16[4096,128]{1,0:T(8,128)(2,1)} %wv.1, s32[1,128]{1,0:T(1,128)} %bitcast.3, s32[4]{0:T(128)} %served_h.1), custom_call_target="tpu_custom_call" | custom-call | tf_op jit(solution)/shard_map/fused_attention/pallas_call | solution.py:309
  46.5 1.9 %copy.11 = bf16[512,512]{1,0:T(8,128)(2,1)} copy(bf16[512,512]{1,0:T(8,128)(2,1)} %get-tuple-element.4) | data formatting | bytes 1048576
  48.4 1.3 %copy.12 = f32[4,4,128]{2,1,0:T(4,128)} copy(f32[4,4,128]{2,1,0:T(4,128)} %get-tuple-element.5) | data formatting | bytes 16384

commit v4 on v3

--- a/solution.py
+++ b/solution.py
@@ -17,7 +17,7 @@
 
 
 def fused(n_attn, nz, tok, gain_h, wq, wk, wv, lens_h, served_h, out, lse_out,
-          gain, lens, served, TOK, X, W, SQ, PSQ, INV, KV, PKV, Q, FR, M, L, ACC, LT, SLOT, RECV, PART,
+          gain, lens, served, TOK, X, W, SQ, PSQ, INV, KV, PKV, Q, FR, M, L, ACC, LT, SLOT, RECV, PART, PB, AL,
           in_sem, w_sem, s_sem, r_sem, kvs_sem, kvr_sem, ls_sem, lr_sem, hop_sem):
     f32 = jnp.float32
     bf16 = jnp.bfloat16
@@ -164,7 +164,20 @@
         for h in range(4):
             Q[j, h * QB:(h + 1) * QB, :] = (acc[:, h * 128:(h + 1) * 128] * inv).astype(bf16)
 
-    def update(i, parts, init):
+    def part_refs(parts):
+        return [(KV if own else PKV).at[j] for own, j in parts]
+
+    def apply(i, hp, parts, pp, al, init):
+        vv = jnp.concatenate([b[1] for b in part_refs(parts)], axis=1)
+        o = jnp.dot(vv, pp, preferred_element_type=f32)
+        cols = slice(hp * 256, (hp + 1) * 256)
+        if not init:
+            o = o + al * ACC[i, :, cols]
+        ACC[i, :, cols] = o
+
+    later = []
+
+    def update(i, parts, init, defer=False):
         cs = LOG2E / HEAD ** 0.5
         n = len(parts)
         oks = []
@@ -174,9 +187,7 @@
             if own and j == i:
                 ok = ok & (sub <= lane)
             oks.append(ok)
-        bufs = [(KV if own else PKV).at[j] for own, j in parts]
-        kk = jnp.concatenate([b[0] for b in bufs], axis=0)
-        vv = jnp.concatenate([b[1] for b in bufs], axis=1)
+        kk = jnp.concatenate([b[0] for b in part_refs(parts)], axis=0)
         for hp in range(2):
             q = Q[i, hp * 256:(hp + 1) * 256, :]
             sc = lax.dot_general(kk, q, (((1,), (1,)), ((), ())), preferred_element_type=f32)
@@ -197,30 +208,51 @@
                 M[i, h:h + 1, :] = mx
                 L[i, h:h + 1, :] = tot
                 halves.append(jnp.concatenate([x.astype(bf16) for x in ps], axis=0))
-            o = jnp.dot(vv, jnp.concatenate(halves, axis=1), preferred_element_type=f32)
-            cols = slice(hp * 256, (hp + 1) * 256)
-            if not init:
-                o = o + jnp.concatenate(als, axis=1) * ACC[i, :, cols]
-            ACC[i, :, cols] = o
+            pp = jnp.concatenate(halves, axis=1)
+            al = None if init else jnp.concatenate(als, axis=1)
+            if defer:
+                slot = len(later)
+                PB[slot, 0:n * QB, :] = pp
+                if not init:
+                    AL[slot:slot + 1, :] = al
+                later.append((i, hp, parts, slot, init))
+            else:
+                apply(i, hp, parts, pp, al, init)
 
     def attend(j):
+        last = j == 0
         for i in range(NC - 1, j + 1, -1):
-            update(i, [(True, j)], False)
+            update(i, [(True, j)], False, last)
         if j + 1 < NC:
             kv_copy(j + 1).wait_recv()
-            update(j + 1, [(True, j), (False, j + 1)], False)
+            update(j + 1, [(True, j), (False, j + 1)], False, last)
         parts = [(True, j)] + [(False, k) for k in range(NC - 1, j, -1)]
         for t in range(0, len(parts), 2):
-            update(j, parts[t:t + 2], t == 0)
+            update(j, parts[t:t + 2], t == 0, last)
+
+    def first_part(c):
+        for k in (1, 4, 5):
+            recv(c, k)
+        PART[c] = jnp.dot(lhs(NC - 1 - c, range(6)), W[:3072, :], preferred_element_type=f32)
+
+    def second_part(c):
+        j = NC - 1 - c
+        recv(c, 7)
+        project(j, PART[c] + jnp.dot(lhs(j, (6, 7)), W[3072:, :], preferred_element_type=f32))
 
     relay_near(NC)
     relay_near(0)
     send_own(2)
-    hop(0)
-    relay_far(NC)
+    for t, k in enumerate(kinds):
+        for cp in w_copies(t, k):
+            cp.wait()
+    first_part(0)
     relay_near(1)
     send_own(3)
-    hop(1)
+    relay_far(NC)
+    first_part(1)
+    hop(0)
+    relay_far(0)
     recv_partner(NC)
     tot = SQ[0]
     for t in range(1, 8):
@@ -228,31 +260,27 @@
     rows_inv = lax.rsqrt(tot * (1.0 / 4096) + EPS)
     for j in range(NC):
         INV[j] = jnp.broadcast_to(jnp.sum(jnp.where(eye, rows_inv[j:j + 1, :], 0.0), axis=1, keepdims=True), (QB, QB))
-    for t, k in enumerate(kinds):
-        for cp in w_copies(t, k):
-            cp.wait()
-
-    for c in range(NC - 1):
-        j = NC - 1 - c
-        relay_far(c)
-        hop(c + 2)
-        recv_partner(c)
-        acc = jnp.dot(lhs(j, range(8)), W[...], preferred_element_type=f32)
-        project(j, acc)
-        if c + 2 < NC:
-            relay_near(c + 2)
-        attend(j)
-
-    c = NC - 1
-    for k in (1, 4, 5):
-        recv(c, k)
-    PART[...] = jnp.dot(lhs(0, range(6)), W[:3072, :], preferred_element_type=f32)
-    relay_far(c)
-    recv(c, 7)
-    project(0, PART[...] + jnp.dot(lhs(0, (6, 7)), W[3072:, :], preferred_element_type=f32))
+    hop(1)
+    second_part(0)
+    relay_near(2)
+    attend(3)
+    first_part(2)
+    hop(2)
+    relay_far(1)
+    relay_near(3)
+    second_part(1)
+    hop(3)
+    attend(2)
+    relay_far(2)
+    first_part(3)
+    second_part(2)
+    relay_far(3)
+    hop(4)
+    attend(1)
+    second_part(3)
     attend(0)
     kv_copy(0).wait_recv()
-    update(0, [(False, 0)], False)
+    update(0, [(False, 0)], False, True)
 
     for i in range(NC):
         LT[i, 0:4, :] = (M[i] + jnp.log2(L[i])) * LN2
@@ -273,6 +301,9 @@
     for d in peers:
         lse_copy(d, a).start()
     RECV[a] = SLOT[a]
+
+    for i, hp, parts, slot, init in later:
+        apply(i, hp, parts, PB[slot, 0:len(parts) * QB, :], None if init else AL[slot:slot + 1, :], init)
 
     for i in range(NC):
         for h in range(4):
@@ -302,7 +333,7 @@
 
 
 def shards(n_attn, nz, tokens, norm_gain, w_query, w_key, value_matrix, doc_lengths, block_server):
-    hbm = pl.BlockSpec(memory_space=pltpu.HBM)
+    hbm = pl.BlockSpec(memory_space=pl.ANY)
     vm = pl.BlockSpec(memory_space=pltpu.VMEM)
     bf16, f32 = jnp.bfloat16, jnp.float32
     dma = pltpu.SemaphoreType.DMA
@@ -331,15 +362,18 @@
             pltpu.VMEM((NC, 8, 128), f32),
             pltpu.VMEM((n_attn, 8, 128), f32),
             pltpu.VMEM((n_attn, 8, 128), f32),
-            pltpu.VMEM((QB, 768), f32),
+            pltpu.VMEM((NC, QB, 768), f32),
+            pltpu.VMEM((12, 2 * QB, 256), bf16),
+            pltpu.VMEM((16, 256), f32),
             dma((4,)), dma((8, 3)), dma((NC + 1, 8)), dma((NC + 1, 8)), dma((NC,)), dma((NC,)),
             dma((n_attn,)), dma((n_attn,)), pltpu.SemaphoreType.REGULAR((5,)),
         ],
         compiler_params=pltpu.CompilerParams(
-            collective_id=0, has_side_effects=True, vmem_limit_bytes=67043328),
+            collective_id=0, has_side_effects=True, vmem_limit_bytes=48 << 20),
         name="fused_attention",
-    )(tokens, norm_gain.reshape(32, 128), w_query, w_key, value_matrix,
-      doc_lengths.reshape(1, 128), block_server)
+    )(*[pltpu.with_memory_space_constraint(t, pltpu.HBM) for t in (
+        tokens, norm_gain.reshape(32, 128), w_query, w_key, value_matrix,
+        doc_lengths.reshape(1, 128), block_server)])
 
 
 def solution(mesh):

time: 50.6 us -> 45.9 us (0.907); the launches traced: 49.7 us -> 45.9 us
  Pallas kernels: 45.9 us -> 43.8 us
  local copies, waits for them, and re-layouts: 3.16 us -> 1.39 us
    pallas_call x1, Pallas kernels: 45.9 us -> 43.8 us  [shards(): pl.pallas_call(functools.partial(fused, n_attn, nz), out_shape=(jax.Shape...]
    unnamed x2, local copies, waits for them, and re-layouts: 3.16 us -> 1.39 us
where the time goes in v4:
time: 45.9 us
  Pallas kernels  43.8 us (95%)
  local copies, waits for them, and re-layouts  1.39 us (3%)
  between operations  0.64 us (1%)
    pallas_call x1, Pallas kernels, shards(): pl.pallas_call(functools.partial(fused, n_attn, nz), out_shape=(jax.Shape...  43.8 us
    unnamed x2, local copies, waits for them, and re-layouts  1.39 us

profile of v4, /device:TPU:2, one launch (start us, length us, event | category | flops | bytes accessed | tf_op | source)
XLA Modules:
  0.0 45.9 jit_solution(8448987760711184161)
XLA Ops:
  0.6 43.8 %fused_attention.1 = (bf16[512,512]{1,0:T(8,128)(2,1)S(1)}, f32[4,4,128]{2,1,0:T(4,128)S(1)}) custom-call(bf16[512,512]{1,0:T(8,128)(2,1)} %tok.1, f32[32,128]{1,0:T(8,128)} %bitcast.2, bf16[4096,512]{1,0:T(8,128)(2,1)} %wq.1, bf16[4096,128]{1,0:T(8,128)(2,1)} %wk.1, bf16[4096,128]{1,0:T(8,128)(2,1)} %wv.1, s32[1,128]{1,0:T(1,128)} %bitcast.3, s32[4]{0:T(128)} %served_h.1), custom_call_target="tpu_custom_call" | custom-call | tf_op jit(solution)/shard_map/fused_attention/pallas_call | solution.py:340
  44.5 0.8 %copy.11 = bf16[512,512]{1,0:T(8,128)(2,1)} copy(bf16[512,512]{1,0:T(8,128)(2,1)S(1)} %get-tuple-element.4) | data formatting | bytes 1048576
  45.3 0.6 %copy.12 = f32[4,4,128]{2,1,0:T(4,128)} copy(f32[4,4,128]{2,1,0:T(4,128)S(1)} %get-tuple-element.5) | data formatting | bytes 16384

commit v5 on v4

--- a/solution.py
+++ b/solution.py
@@ -17,7 +17,7 @@
 
 
 def fused(n_attn, nz, tok, gain_h, wq, wk, wv, lens_h, served_h, out, lse_out,
-          gain, lens, served, TOK, X, W, SQ, PSQ, INV, KV, PKV, Q, FR, M, L, ACC, LT, SLOT, RECV, PART, PB, AL,
+          gain, lens, served, TOK, X, W, SQ, PSQ, INV, KV, PKV, Q, FR, M, L, LT, SLOT, RECV, PART, PB, AL,
           in_sem, w_sem, s_sem, r_sem, kvs_sem, kvr_sem, ls_sem, lr_sem, hop_sem):
     f32 = jnp.float32
     bf16 = jnp.bfloat16
@@ -42,8 +42,12 @@
     nxt = lax.rem(a + 1, n_attn)
     prv = lax.rem(a + n_attn - 1, n_attn)
 
+    blk = lambda j: pl.ds(j * QB, QB)
     small = [pltpu.make_async_copy(src, dst, in_sem.at[i])
-             for i, (src, dst) in enumerate(((tok, TOK), (gain_h, gain), (lens_h, lens), (served_h, served)))]
+             for i, (src, dst) in enumerate((
+                 (gain_h, gain), (tok.at[blk(NC - 1), :], TOK.at[blk(NC - 1), :]),
+                 (tok.at[pl.ds(0, (NC - 1) * QB), :], TOK.at[pl.ds(0, (NC - 1) * QB), :]),
+                 (lens_h, lens), (served_h, served)))]
     for cp in small:
         cp.start()
 
@@ -63,13 +67,12 @@
     for t, k in enumerate(kinds):
         for cp in w_copies(t, k):
             cp.start()
-    for cp in small:
-        cp.wait()
 
     lane = lax.broadcasted_iota(jnp.int32, (QB, QB), 1).astype(f32)
     sub = lax.broadcasted_iota(jnp.int32, (QB, QB), 0).astype(f32)
     eye = sub == lane
 
+    small[0].wait()
     g = jnp.concatenate([gain[pl.ds(4 * p + u, 1), :] for u in range(4)], axis=1)
 
     def scale_rows(n, carry):
@@ -80,12 +83,9 @@
         PSQ[r, :] = (x2[:, 0:128] + x2[:, 128:256]) + (x2[:, 256:384] + x2[:, 384:512])
         return carry
 
-    lax.fori_loop(0, NC * QB // 32, scale_rows, 0)
-    for j in range(NC):
-        col = jnp.sum(PSQ[j * QB:(j + 1) * QB, :], axis=1, keepdims=True)
-        SQ[0, j:j + 1, :] = jnp.sum(jnp.where(eye, col, 0.0), axis=0, keepdims=True)
-        SQ[0, NC + j:NC + j + 1, :] = jnp.zeros((1, QB), f32)
-
+    per = QB // 32
+    small[1].wait()
+    lax.fori_loop((NC - 1) * per, NC * per, scale_rows, 0)
     pl.semaphore_wait(barrier, 9)
 
     def hop_signal(k):
@@ -111,32 +111,61 @@
             device_id=(a, dst_proj), device_id_type=MESH)
 
     def send_own(c):
+        rc(c, 1, 0, partner).start()
         rc(c, 2, 0, ahead).start()
         rc(c, 3, 0, behind).start()
-        rc(c, 1, 0, partner).start()
 
     def recv(c, kind):
         rc(c, kind, kind, partner).wait_recv()
 
+    def fcopy(c, side):
+        if c == NC:
+            src, dst = SQ.at[2], SQ.at[6]
+        else:
+            r = pl.ds((NC - 1 - c) * QB + side * (QB // 2), QB // 2)
+            src, dst = X.at[2 + side, r, :], X.at[6, r, :]
+        k = 6 + 2 * side
+        return pltpu.make_async_remote_copy(
+            src_ref=src, dst_ref=dst, send_sem=s_sem.at[c, k], recv_sem=r_sem.at[c, k],
+            device_id=(a, behind if side else ahead), device_id_type=MESH)
+
+    def sides(c):
+        return (0,) if c == NC else (0, 1)
+
     def relay_near(c):
         recv(c, 2)
-        rc(c, 6, 2, ahead).start()
+        recv(c, 3)
         rc(c, 4, 2, partner).start()
-        recv(c, 3)
         rc(c, 5, 3, partner).start()
 
+    def forward(c):
+        for t in sides(c):
+            fcopy(c, t).start()
+
     def relay_far(c):
-        recv(c, 6)
+        for t in sides(c):
+            fcopy(c, t).wait_recv()
         rc(c, 7, 6, partner).start()
 
     def recv_partner(c):
         for k in (1, 4, 5, 7):
             recv(c, k)
 
+    send_own(0)
+    small[2].wait()
+    lax.fori_loop(0, (NC - 1) * per, scale_rows, 0)
+    for j in range(NC):
+        col = jnp.sum(PSQ[j * QB:(j + 1) * QB, :], axis=1, keepdims=True)
+        SQ[0, j:j + 1, :] = jnp.sum(jnp.where(eye, col, 0.0), axis=0, keepdims=True)
+        SQ[0, NC + j:NC + j + 1, :] = jnp.zeros((1, QB), f32)
     send_own(NC)
-    send_own(0)
-    send_own(1)
-
+
+    @pl.when(core == 0)
+    def _():
+        send_own(1)
+
+    small[3].wait()
+    small[4].wait()
     ln = jnp.broadcast_to(lens[...].astype(f32), (8, 128))
     cum = ln
     for k in (1, 2, 4, 8, 16, 32, 64):
@@ -156,28 +185,23 @@
     def lhs(j, ks):
         return jnp.concatenate([X[t, j * QB:(j + 1) * QB, :] for t in ks], axis=1)
 
-    def project(j, acc):
+    def project_kv(j, acc):
         inv = INV[j]
-        KV[j, 0] = (acc[:, 512:640] * inv).astype(bf16)
-        KV[j, 1] = jnp.transpose(acc[:, 640:768] * inv).astype(bf16)
+        KV[j, 0] = (acc[:, 0:128] * inv).astype(bf16)
+        KV[j, 1] = jnp.transpose(acc[:, 128:256] * inv).astype(bf16)
         kv_copy(j).start()
+
+    def project_q(j, acc):
+        inv = INV[j]
         for h in range(4):
             Q[j, h * QB:(h + 1) * QB, :] = (acc[:, h * 128:(h + 1) * 128] * inv).astype(bf16)
 
     def part_refs(parts):
         return [(KV if own else PKV).at[j] for own, j in parts]
 
-    def apply(i, hp, parts, pp, al, init):
-        vv = jnp.concatenate([b[1] for b in part_refs(parts)], axis=1)
-        o = jnp.dot(vv, pp, preferred_element_type=f32)
-        cols = slice(hp * 256, (hp + 1) * 256)
-        if not init:
-            o = o + al * ACC[i, :, cols]
-        ACC[i, :, cols] = o
-
     later = []
 
-    def update(i, parts, init, defer=False):
+    def update(i, parts, init):
         cs = LOG2E / HEAD ** 0.5
         n = len(parts)
         oks = []
@@ -210,25 +234,23 @@
                 halves.append(jnp.concatenate([x.astype(bf16) for x in ps], axis=0))
             pp = jnp.concatenate(halves, axis=1)
             al = None if init else jnp.concatenate(als, axis=1)
-            if defer:
-                slot = len(later)
-                PB[slot, 0:n * QB, :] = pp
-                if not init:
-                    AL[slot:slot + 1, :] = al
-                later.append((i, hp, parts, slot, init))
-            else:
-                apply(i, hp, parts, pp, al, init)
-
-    def attend(j):
-        last = j == 0
+            slot = len(later)
+            PB[slot, 0:n * QB, :] = pp
+            if not init:
+                AL[slot:slot + 1, :] = al
+            later.append((i, hp, parts, slot, init))
+
+    def attend_old(j):
         for i in range(NC - 1, j + 1, -1):
-            update(i, [(True, j)], False, last)
+            update(i, [(True, j)], False)
         if j + 1 < NC:
             kv_copy(j + 1).wait_recv()
-            update(j + 1, [(True, j), (False, j + 1)], False, last)
+            update(j + 1, [(True, j), (False, j + 1)], False)
+
+    def attend_new(j):
         parts = [(True, j)] + [(False, k) for k in range(NC - 1, j, -1)]
         for t in range(0, len(parts), 2):
-            update(j, parts[t:t + 2], t == 0, last)
+            update(j, parts[t:t + 2], t == 0)
 
     def first_part(c):
         for k in (1, 4, 5):
@@ -238,21 +260,30 @@
     def second_part(c):
         j = NC - 1 - c
         recv(c, 7)
-        project(j, PART[c] + jnp.dot(lhs(j, (6, 7)), W[3072:, :], preferred_element_type=f32))
+        x = lhs(j, (6, 7))
+        project_kv(j, PART[c, :, 512:768] + jnp.dot(x, W[3072:, 512:768], preferred_element_type=f32))
+        project_q(j, PART[c, :, 0:512] + jnp.dot(x, W[3072:, 0:512], preferred_element_type=f32))
+
+    relay_near(0)
+
+    @pl.when(core == 1)
+    def _():
+        send_own(1)
 
     relay_near(NC)
-    relay_near(0)
+    forward(NC)
+    forward(0)
     send_own(2)
     for t, k in enumerate(kinds):
         for cp in w_copies(t, k):
             cp.wait()
+    relay_near(1)
     first_part(0)
-    relay_near(1)
+    relay_far(NC)
+    relay_far(0)
+    forward(1)
     send_own(3)
-    relay_far(NC)
     first_part(1)
-    hop(0)
-    relay_far(0)
     recv_partner(NC)
     tot = SQ[0]
     for t in range(1, 8):
@@ -260,27 +291,33 @@
     rows_inv = lax.rsqrt(tot * (1.0 / 4096) + EPS)
     for j in range(NC):
         INV[j] = jnp.broadcast_to(jnp.sum(jnp.where(eye, rows_inv[j:j + 1, :], 0.0), axis=1, keepdims=True), (QB, QB))
+    second_part(0)
+    attend_new(3)
+    hop(0)
+    relay_near(2)
+    relay_far(1)
+    forward(2)
+    first_part(2)
+    second_part(1)
+    attend_old(2)
+    attend_new(2)
     hop(1)
-    second_part(0)
-    relay_near(2)
-    attend(3)
-    first_part(2)
-    hop(2)
-    relay_far(1)
     relay_near(3)
-    second_part(1)
-    hop(3)
-    attend(2)
+    forward(3)
     relay_far(2)
     first_part(3)
+    hop(2)
     second_part(2)
     relay_far(3)
+    attend_old(1)
+    hop(3)
+    second_part(3)
+    attend_new(1)
+    attend_old(0)
+    attend_new(0)
     hop(4)
-    attend(1)
-    second_part(3)
-    attend(0)
     kv_copy(0).wait_recv()
-    update(0, [(False, 0)], False, True)
+    update(0, [(False, 0)], False)
 
     for i in range(NC):
         LT[i, 0:4, :] = (M[i] + jnp.log2(L[i])) * LN2
@@ -302,13 +339,17 @@
         lse_copy(d, a).start()
     RECV[a] = SLOT[a]
 
-    for i, hp, parts, slot, init in later:
-        apply(i, hp, parts, PB[slot, 0:len(parts) * QB, :], None if init else AL[slot:slot + 1, :], init)
-
     for i in range(NC):
-        for h in range(4):
-            o = ACC[i, :, h * 128:(h + 1) * 128] / L[i, h:h + 1, :]
-            out[i * QB:(i + 1) * QB, h * 128:(h + 1) * 128] = jnp.transpose(o).astype(bf16)
+        for hp in range(2):
+            o = None
+            for _, _, parts, slot, init in [t for t in later if t[:2] == (i, hp)]:
+                vv = jnp.concatenate([b[1] for b in part_refs(parts)], axis=1)
+                d = jnp.dot(vv, PB[slot, 0:len(parts) * QB, :], preferred_element_type=f32)
+                o = d if init else AL[slot:slot + 1, :] * o + d
+            for u in range(2):
+                h = 2 * hp + u
+                res = o[:, u * 128:(u + 1) * 128] / L[i, h:h + 1, :]
+                out[i * QB:(i + 1) * QB, h * 128:(h + 1) * 128] = jnp.transpose(res).astype(bf16)
 
     for d in peers:
         lse_copy(d, d).wait_recv()
@@ -324,8 +365,10 @@
         lse_out[i] = res[i]
 
     for c in range(NC + 1):
-        for k in (1, 2, 3, 4, 5, 6, 7):
+        for k in (1, 2, 3, 4, 5, 7):
             rc(c, k, k, partner).wait_send()
+        for t in sides(c):
+            fcopy(c, t).wait_send()
     for j in range(NC):
         kv_copy(j).wait_send()
     for d in peers:
@@ -358,14 +401,13 @@
             pltpu.VMEM((8, QB), f32),
             pltpu.VMEM((NC, 4, 128), f32),
             pltpu.VMEM((NC, 4, 128), f32),
-            pltpu.VMEM((NC, 128, 4 * QB), f32),
             pltpu.VMEM((NC, 8, 128), f32),
             pltpu.VMEM((n_attn, 8, 128), f32),
             pltpu.VMEM((n_attn, 8, 128), f32),
             pltpu.VMEM((NC, QB, 768), f32),
-            pltpu.VMEM((12, 2 * QB, 256), bf16),
-            pltpu.VMEM((16, 256), f32),
-            dma((4,)), dma((8, 3)), dma((NC + 1, 8)), dma((NC + 1, 8)), dma((NC,)), dma((NC,)),
+            pltpu.VMEM((26, 2 * QB, 256), bf16),
+            pltpu.VMEM((32, 256), f32),
+            dma((5,)), dma((8, 3)), dma((NC + 1, 9)), dma((NC + 1, 9)), dma((NC,)), dma((NC,)),
             dma((n_attn,)), dma((n_attn,)), pltpu.SemaphoreType.REGULAR((5,)),
         ],
         compiler_params=pltpu.CompilerParams(

time: 45.9 us -> 44.8 us (0.976)
  the two profiles are of different devices: /device:TPU:2 before, /device:TPU:1 now
where the time goes in v5:
time: 44.8 us; the launch traced here: 44.7 us
  Pallas kernels  42.6 us (95%)
  local copies, waits for them, and re-layouts  1.39 us (3%)
  between operations  0.64 us (1%)
    pallas_call x1, Pallas kernels, shards(): pl.pallas_call(functools.partial(fused, n_attn, nz), out_shape=(jax.Shape...  42.6 us
    unnamed x2, local copies, waits for them, and re-layouts  1.39 us

profile of v5, /device:TPU:1, one launch (start us, length us, event | category | flops | bytes accessed | tf_op | source)
XLA Modules:
  0.0 44.7 jit_solution(6724341215381687066)
XLA Ops:
  0.6 42.6 %fused_attention.1 = (bf16[512,512]{1,0:T(8,128)(2,1)S(1)}, f32[4,4,128]{2,1,0:T(4,128)S(1)}) custom-call(bf16[512,512]{1,0:T(8,128)(2,1)} %tok.1, f32[32,128]{1,0:T(8,128)} %bitcast.2, bf16[4096,512]{1,0:T(8,128)(2,1)} %wq.1, bf16[4096,128]{1,0:T(8,128)(2,1)} %wk.1, bf16[4096,128]{1,0:T(8,128)(2,1)} %wv.1, s32[1,128]{1,0:T(1,128)} %bitcast.3, s32[4]{0:T(128)} %served_h.1), custom_call_target="tpu_custom_call" | custom-call | tf_op jit(solution)/shard_map/fused_attention/pallas_call | solution.py:383
  43.3 0.8 %copy.11 = bf16[512,512]{1,0:T(8,128)(2,1)} copy(bf16[512,512]{1,0:T(8,128)(2,1)S(1)} %get-tuple-element.4) | data formatting | bytes 1048576
  44.1 0.6 %copy.12 = f32[4,4,128]{2,1,0:T(4,128)} copy(f32[4,4,128]{2,1,0:T(4,128)S(1)} %get-tuple-element.5) | data formatting | bytes 16384

commit v6 on v5

--- a/solution.py
+++ b/solution.py
@@ -14,6 +14,7 @@
 LN2 = 0.6931471805599453
 MESH = pl.DeviceIdType.MESH
 NC = 4
+PIECES = 4
 
 
 def fused(n_attn, nz, tok, gain_h, wq, wk, wv, lens_h, served_h, out, lse_out,
@@ -64,9 +65,6 @@
                 pltpu.make_async_copy(wk.at[r, :], W.at[d, pl.ds(512, 128)], w_sem.at[t, 1]),
                 pltpu.make_async_copy(wv.at[r, :], W.at[d, pl.ds(640, 128)], w_sem.at[t, 2]))
 
-    for t, k in enumerate(kinds):
-        for cp in w_copies(t, k):
-            cp.start()
 
     lane = lax.broadcasted_iota(jnp.int32, (QB, QB), 1).astype(f32)
     sub = lax.broadcasted_iota(jnp.int32, (QB, QB), 0).astype(f32)
@@ -110,10 +108,38 @@
             send_sem=s_sem.at[c, kind], recv_sem=r_sem.at[c, kind],
             device_id=(a, dst_proj), device_id_type=MESH)
 
+    def share(c, kind, src_kind):
+        if c == NC:
+            rc(c, kind, src_kind, partner).start()
+            return
+        step = QB // PIECES
+        for t in range(PIECES):
+            r = pl.ds((NC - 1 - c) * QB + t * step, step)
+            pltpu.make_async_remote_copy(
+                src_ref=X.at[src_kind, r, :], dst_ref=X.at[kind, r, :],
+                send_sem=s_sem.at[c, kind], recv_sem=r_sem.at[c, kind],
+                device_id=(a, partner), device_id_type=MESH).start()
+
+    def half_copy(side, piece):
+        r = pl.ds((side ^ piece) * (QB // 2), QB // 2)
+        k = 2 + side if piece == 0 else 9 + side
+        return pltpu.make_async_remote_copy(
+            src_ref=X.at[0, r, :], dst_ref=X.at[2 + side, r, :],
+            send_sem=s_sem.at[NC - 1, k], recv_sem=r_sem.at[NC - 1, k],
+            device_id=(a, behind if side else ahead), device_id_type=MESH)
+
     def send_own(c):
-        rc(c, 1, 0, partner).start()
+        if c != 0:
+            share(c, 1, 0)
+        if c == NC - 1:
+            for piece in range(2):
+                for side in range(2):
+                    half_copy(side, piece).start()
+            return
         rc(c, 2, 0, ahead).start()
         rc(c, 3, 0, behind).start()
+        if c == 0:
+            share(c, 1, 0)
 
     def recv(c, kind):
         rc(c, kind, kind, partner).wait_recv()
@@ -132,11 +158,20 @@
     def sides(c):
         return (0,) if c == NC else (0, 1)
 
+    def relay_first(c):
+        for side in range(2):
+            half_copy(side, 0).wait_recv()
+            fcopy(c, side).start()
+
     def relay_near(c):
-        recv(c, 2)
-        recv(c, 3)
-        rc(c, 4, 2, partner).start()
-        rc(c, 5, 3, partner).start()
+        if c == NC - 1:
+            half_copy(0, 1).wait_recv()
+            half_copy(1, 1).wait_recv()
+        else:
+            recv(c, 2)
+            recv(c, 3)
+        share(c, 4, 2)
+        share(c, 5, 3)
 
     def forward(c):
         for t in sides(c):
@@ -145,13 +180,16 @@
     def relay_far(c):
         for t in sides(c):
             fcopy(c, t).wait_recv()
-        rc(c, 7, 6, partner).start()
+        share(c, 7, 6)
 
     def recv_partner(c):
         for k in (1, 4, 5, 7):
             recv(c, k)
 
     send_own(0)
+    for t, k in enumerate(kinds):
+        for cp in w_copies(t, k):
+            cp.start()
     small[2].wait()
     lax.fori_loop(0, (NC - 1) * per, scale_rows, 0)
     for j in range(NC):
@@ -177,9 +215,9 @@
         first = jnp.max(jnp.where(starts <= pos, starts, 0.0), axis=0, keepdims=True)
         FR[i:i + 1, :] = first - base
 
-    def kv_copy(j):
+    def kv_copy(j, t):
         return pltpu.make_async_remote_copy(
-            src_ref=KV.at[j], dst_ref=PKV.at[j], send_sem=kvs_sem.at[j], recv_sem=kvr_sem.at[j],
+            src_ref=KV.at[j, t], dst_ref=PKV.at[j, t], send_sem=kvs_sem.at[j, t], recv_sem=kvr_sem.at[j, t],
             device_id=(nxt, p), device_id_type=MESH)
 
     def lhs(j, ks):
@@ -188,8 +226,9 @@
     def project_kv(j, acc):
         inv = INV[j]
         KV[j, 0] = (acc[:, 0:128] * inv).astype(bf16)
+        kv_copy(j, 0).start()
         KV[j, 1] = jnp.transpose(acc[:, 128:256] * inv).astype(bf16)
-        kv_copy(j).start()
+        kv_copy(j, 1).start()
 
     def project_q(j, acc):
         inv = INV[j]
@@ -244,7 +283,7 @@
         for i in range(NC - 1, j + 1, -1):
             update(i, [(True, j)], False)
         if j + 1 < NC:
-            kv_copy(j + 1).wait_recv()
+            kv_copy(j + 1, 0).wait_recv()
             update(j + 1, [(True, j), (False, j + 1)], False)
 
     def attend_new(j):
@@ -298,12 +337,12 @@
     relay_far(1)
     forward(2)
     first_part(2)
+    relay_first(3)
     second_part(1)
     attend_old(2)
     attend_new(2)
     hop(1)
     relay_near(3)
-    forward(3)
     relay_far(2)
     first_part(3)
     hop(2)
@@ -316,7 +355,7 @@
     attend_old(0)
     attend_new(0)
     hop(4)
-    kv_copy(0).wait_recv()
+    kv_copy(0, 0).wait_recv()
     update(0, [(False, 0)], False)
 
     for i in range(NC):
@@ -339,6 +378,8 @@
         lse_copy(d, a).start()
     RECV[a] = SLOT[a]
 
+    for j in range(NC):
+        kv_copy(j, 1).wait_recv()
     for i in range(NC):
         for hp in range(2):
             o = None
@@ -365,12 +406,16 @@
         lse_out[i] = res[i]
 
     for c in range(NC + 1):
-        for k in (1, 2, 3, 4, 5, 7):
+        for k in (1, 4, 5, 7) if c == NC - 1 else (1, 2, 3, 4, 5, 7):
             rc(c, k, k, partner).wait_send()
         for t in sides(c):
             fcopy(c, t).wait_send()
+    for side in range(2):
+        for piece in range(2):
+            half_copy(side, piece).wait_send()
     for j in range(NC):
-        kv_copy(j).wait_send()
+        for t in range(2):
+            kv_copy(j, t).wait_send()
     for d in peers:
         lse_copy(d, a).wait_send()
 
@@ -407,7 +452,7 @@
             pltpu.VMEM((NC, QB, 768), f32),
             pltpu.VMEM((26, 2 * QB, 256), bf16),
             pltpu.VMEM((32, 256), f32),
-            dma((5,)), dma((8, 3)), dma((NC + 1, 9)), dma((NC + 1, 9)), dma((NC,)), dma((NC,)),
+            dma((5,)), dma((8, 3)), dma((NC + 1, 11)), dma((NC + 1, 11)), dma((NC, 2)), dma((NC, 2)),
             dma((n_attn,)), dma((n_attn,)), pltpu.SemaphoreType.REGULAR((5,)),
         ],
         compiler_params=pltpu.CompilerParams(

time: 44.8 us -> 43.7 us (0.975)
  the two profiles are of different devices: /device:TPU:1 before, /device:TPU:2 now
where the time goes in v6:
time: 43.7 us; the launch traced here: 43.5 us
  Pallas kernels  41.5 us (95%)
  local copies, waits for them, and re-layouts  1.39 us (3%)
  between operations  0.64 us (1%)
    pallas_call x1, Pallas kernels, shards(): pl.pallas_call(functools.partial(fused, n_attn, nz), out_shape=(jax.Shape...  41.5 us
    unnamed x2, local copies, waits for them, and re-layouts  1.39 us

profile of v6, /device:TPU:2, one launch (start us, length us, event | category | flops | bytes accessed | tf_op | source)
XLA Modules:
  0.0 43.5 jit_solution(5878099046476679561)
XLA Ops:
  0.6 41.5 %fused_attention.1 = (bf16[512,512]{1,0:T(8,128)(2,1)S(1)}, f32[4,4,128]{2,1,0:T(4,128)S(1)}) custom-call(bf16[512,512]{1,0:T(8,128)(2,1)} %tok.1, f32[32,128]{1,0:T(8,128)} %bitcast.2, bf16[4096,512]{1,0:T(8,128)(2,1)} %wq.1, bf16[4096,128]{1,0:T(8,128)(2,1)} %wk.1, bf16[4096,128]{1,0:T(8,128)(2,1)} %wv.1, s32[1,128]{1,0:T(1,128)} %bitcast.3, s32[4]{0:T(128)} %served_h.1), custom_call_target="tpu_custom_call" | custom-call | tf_op jit(solution)/shard_map/fused_attention/pallas_call | solution.py:428
  42.1 0.8 %copy.11 = bf16[512,512]{1,0:T(8,128)(2,1)} copy(bf16[512,512]{1,0:T(8,128)(2,1)S(1)} %get-tuple-element.4) | data formatting | bytes 1048576
  42.9 0.6 %copy.12 = f32[4,4,128]{2,1,0:T(4,128)} copy(f32[4,4,128]{2,1,0:T(4,128)S(1)} %get-tuple-element.5) | data formatting | bytes 16384

commit v7 on v6

--- a/solution.py
+++ b/solution.py
@@ -337,8 +337,8 @@
     relay_far(1)
     forward(2)
     first_part(2)
+    second_part(1)
     relay_first(3)
-    second_part(1)
     attend_old(2)
     attend_new(2)
     hop(1)
@@ -420,12 +420,20 @@
         lse_copy(d, a).wait_send()
 
 
+def store(a_ref, b_ref, a_out, b_out, sem):
+    copies = [pltpu.make_async_copy(a_ref, a_out, sem.at[0]), pltpu.make_async_copy(b_ref, b_out, sem.at[1])]
+    for cp in copies:
+        cp.start()
+    for cp in copies:
+        cp.wait()
+
+
 def shards(n_attn, nz, tokens, norm_gain, w_query, w_key, value_matrix, doc_lengths, block_server):
     hbm = pl.BlockSpec(memory_space=pl.ANY)
     vm = pl.BlockSpec(memory_space=pltpu.VMEM)
     bf16, f32 = jnp.bfloat16, jnp.float32
     dma = pltpu.SemaphoreType.DMA
-    return pl.pallas_call(
+    res = pl.pallas_call(
         functools.partial(fused, n_attn, nz),
         out_shape=(jax.ShapeDtypeStruct((512, 512), bf16), jax.ShapeDtypeStruct((4, 4, 128), f32)),
         in_specs=[hbm] * 7,
@@ -461,6 +469,16 @@
     )(*[pltpu.with_memory_space_constraint(t, pltpu.HBM) for t in (
         tokens, norm_gain.reshape(32, 128), w_query, w_key, value_matrix,
         doc_lengths.reshape(1, 128), block_server)])
+    hbm = pl.BlockSpec(memory_space=pltpu.HBM)
+    return pl.pallas_call(
+        store,
+        out_shape=(jax.ShapeDtypeStruct((512, 512), bf16), jax.ShapeDtypeStruct((4, 4, 128), f32)),
+        in_specs=[vm, vm],
+        out_specs=(hbm, hbm),
+        scratch_shapes=[dma((2,))],
+        compiler_params=pltpu.CompilerParams(vmem_limit_bytes=8 << 20),
+        name="store_out",
+    )(*res)
 
 
 def solution(mesh):

time: 43.7 us -> 43.1 us (0.986)
  local copies, waits for them, and re-layouts: 1.39 us -> 0 us
  Pallas kernels: 41.5 us -> 42.3 us
    unnamed x2 -> x0, local copies, waits for them, and re-layouts: 1.39 us -> none
    pallas_call x0 -> x1, Pallas kernels: none -> 0.81 us  [shards(): pl.pallas_call(store, out_shape=(jax.ShapeDtypeStruct((512, 512), bf16),...]
where the time goes in v7:
time: 43.1 us; the launch traced here: 42.9 us
  Pallas kernels  42.3 us (98%)
  between operations  0.64 us (1%)
    pallas_call x1, Pallas kernels, shards(): pl.pallas_call(functools.partial(fused, n_attn, nz), out_shape=(jax.Shape...  41.5 us

profile of v7, /device:TPU:2, one launch (start us, length us, event | category | flops | bytes accessed | tf_op | source)
XLA Modules:
  0.0 42.9 jit_solution(5110916821353970861)
XLA Ops:
  0.6 41.5 %fused_attention.1 = (bf16[512,512]{1,0:T(8,128)(2,1)S(1)}, f32[4,4,128]{2,1,0:T(4,128)S(1)}) custom-call(bf16[512,512]{1,0:T(8,128)(2,1)} %tok.1, f32[32,128]{1,0:T(8,128)} %bitcast.2, bf16[4096,512]{1,0:T(8,128)(2,1)} %wq.1, bf16[4096,128]{1,0:T(8,128)(2,1)} %wk.1, bf16[4096,128]{1,0:T(8,128)(2,1)} %wv.1, s32[1,128]{1,0:T(1,128)} %bitcast.3, s32[4]{0:T(128)} %served_h.1), custom_call_target="tpu_custom_call" | custom-call | tf_op jit(solution)/shard_map/fused_attention/pallas_call | solution.py:436
  42.1 0.8 %store_out.1 = (bf16[512,512]{1,0:T(8,128)(2,1)}, f32[4,4,128]{2,1,0:T(4,128)}) custom-call(bf16[512,512]{1,0:T(8,128)(2,1)S(1)} %get-tuple-element.4.a_ref, f32[4,4,128]{2,1,0:T(4,128)S(1)} %get-tuple-element.5.b_ref), custom_call_target="tpu_custom_call" | custom-call | tf_op jit(solution)/shard_map/store_out/pallas_call | solution.py:473
